TPU v7x, 32 devices: a whole 2x2x4 slice. The times are simulated.
32 devices in a mesh: gx: 16 (over z, y, x), gy: 2 (over core).
Axes of the slice: x: 2, y: 2, z: 4, core: 2. Of those that a mesh axis runs over, the one named last changes fastest.
Arguments:
- right_side: float32 [64, 128, 128], P('gx', 'gy'), may hold values from -12 to 12
- phase: int32 [64, 128, 128], P('gx', 'gy'), may hold values from 0 to 1, as said below
Outputs:
- scaled_solution: float32 [64, 128, 128], P('gx', 'gy')
- residual: float32 [64, 128, 128], P('gx', 'gy')
Inputs may be any that keep to these rules, and one draw needn't show every extreme that they name: `phase`: constant on each 2 x 2 x 2 block of cells that starts at even indices.
All inputs are finite; a program needn't handle non-finite values.
Results may differ from a plain program's by a relative error of at most 0.0024.
Values may be sent and summed in bfloat16 or wider, within the bound.
A program may use at most 64 MiB of HBM per device.

v0:
```python
import jax
import jax.numpy as jnp
from jax import lax
from jax.sharding import PartitionSpec as P

LEVELS = 6
NU = 2
COARSE_SWEEPS = 6


OMEGA = 0.8


def padded(block, sides, width):
    for axis, dim in sides:
        count = lax.axis_size(axis)
        forward = [(i, i + 1) for i in range(count - 1)]
        backward = [(target, source) for source, target in forward]
        low = lax.ppermute(
            lax.slice_in_dim(block, block.shape[dim] - width, None, axis=dim), axis, forward
        )
        high = lax.ppermute(lax.slice_in_dim(block, 0, width, axis=dim), axis, backward)
        block = jnp.concatenate([low, block, high], axis=dim)
    return block


def from_behind(block, axis, distance):
    devices = range(lax.axis_size(axis))
    route = [(i - distance, i) for i in devices if i - distance in devices]
    return lax.ppermute(block, axis, route)


def partner_2(value, axis, stride):
    mask = 2**stride
    pairs = [(source, source ^ mask) for source in range(lax.axis_size(axis))]
    return lax.ppermute(value, axis, pairs)


def harmonic(lower_cell, upper_cell):
    lower_value = jnp.where(lower_cell > 0, lower_cell, upper_cell)
    upper_value = jnp.where(upper_cell > 0, upper_cell, lower_cell)
    return (2.0 * lower_value * upper_value / (lower_value + upper_value)).astype(jnp.bfloat16)


def face_table(widened):
    face_x = harmonic(widened[:-1, 1:-1], widened[1:, 1:-1])
    face_y = harmonic(widened[1:-1, :-1], widened[1:-1, 1:])
    interior = jnp.pad(widened[1:-1, 1:-1], ((0, 0), (0, 0), (1, 1)), mode="edge")
    face_z = harmonic(interior[:, :, :-1], interior[:, :, 1:])
    return (face_x, face_y, face_z)


def pair_sum(values, dimension):
    dims_list = list(values.shape)
    dims_list[dimension : dimension + 1] = [dims_list[dimension] // 2, 2]
    return jnp.sum(values.reshape(dims_list), axis=dimension + 1)


def coarsen(faces):
    face_x, face_y, face_z = faces
    new_x = 0.25 * pair_sum(pair_sum(face_x.astype(jnp.float32)[0::2], 1), 2)
    new_y = 0.25 * pair_sum(pair_sum(face_y.astype(jnp.float32)[:, 0::2], 0), 2)
    new_z = 0.25 * pair_sum(pair_sum(face_z.astype(jnp.float32)[:, :, 0::2], 0), 1)
    return (new_x.astype(jnp.bfloat16), new_y.astype(jnp.bfloat16), new_z.astype(jnp.bfloat16))


def restrict(remainder):
    return 0.5 * pair_sum(pair_sum(pair_sum(remainder, 0), 1), 2)


def prolong(coarse):
    return jnp.repeat(jnp.repeat(jnp.repeat(coarse, 2, 0), 2, 1), 2, 2)


def centre_weight(faces):
    face_x, face_y, face_z = faces
    return (
        face_x[:-1].astype(jnp.float32)
        + face_x[1:].astype(jnp.float32)
        + face_y[:, :-1].astype(jnp.float32)
        + face_y[:, 1:].astype(jnp.float32)
        + face_z[:, :, :-1].astype(jnp.float32)
        + face_z[:, :, 1:].astype(jnp.float32)
    )


def weighted(widened, faces):
    face_x, face_y, face_z = faces
    z_padded = jnp.pad(widened[1:-1, 1:-1], ((0, 0), (0, 0), (1, 1)))
    return (
        face_x[:-1] * widened[:-2, 1:-1]
        + face_x[1:] * widened[2:, 1:-1]
        + face_y[:, :-1] * widened[1:-1, :-2]
        + face_y[:, 1:] * widened[1:-1, 2:]
        + face_z[:, :, :-1] * z_padded[:, :, :-2]
        + face_z[:, :, 1:] * z_padded[:, :, 2:]
    )


def widen(field, stride):
    lateral = padded(field, (("gy", 1),), 1)
    lower_plane = from_behind(field[-1:], "gx", stride)
    upper_plane = from_behind(field[:1], "gx", -stride)
    lower_plane = jnp.pad(lower_plane, ((0, 0), (1, 1), (0, 0)))
    upper_plane = jnp.pad(upper_plane, ((0, 0), (1, 1), (0, 0)))
    return jnp.concatenate([lower_plane, lateral, upper_plane], axis=0)


def join_halves(own_part, partner, upper_half, drop_top):
    first_part = jnp.where(upper_half == 1, partner, own_part)
    second_part = jnp.where(upper_half == 1, own_part, partner)
    if drop_top:
        first_part = first_part[:-1]
    return jnp.concatenate([first_part, second_part], axis=0)


def merged_cycle(remainder, faces, level_index, stride):
    bit_index = stride.bit_length() - 1
    face_x, face_y, face_z = faces
    own_part = (
        remainder,
        face_x.astype(jnp.float32),
        face_y.astype(jnp.float32),
        face_z.astype(jnp.float32),
    )
    partner = partner_2((own_part[0], own_part[1], own_part[2], own_part[3]), "gx", bit_index)
    upper_half = lax.axis_index("gx") // stride % 2
    merged_rest = join_halves(own_part[0], partner[0], upper_half, False)
    merged_x = join_halves(own_part[1], partner[1], upper_half, True).astype(jnp.bfloat16)
    merged_y = join_halves(own_part[2], partner[2], upper_half, False).astype(jnp.bfloat16)
    merged_z = join_halves(own_part[3], partner[3], upper_half, False).astype(jnp.bfloat16)
    coarse = cycle(
        restrict(merged_rest),
        coarsen((merged_x, merged_y, merged_z)),
        level_index + 1,
        stride * 2,
        False,
    )
    refined = prolong(coarse)
    planes = remainder.shape[0]
    return lax.dynamic_slice_in_dim(refined, upper_half * planes, planes, 0)


def cycle(source, faces, level_index, stride, whole_x):
    centre = centre_weight(faces)

    def operate(field):
        return centre * field - weighted(widen(field, stride), faces)

    def smooth(field):
        return field + OMEGA * (source - operate(field)) / centre

    field = OMEGA * source / centre
    if level_index == LEVELS:
        for repeat in range(COARSE_SWEEPS - 1):
            field = smooth(field)
        return field
    field = smooth(field)
    remainder = source - operate(field)
    if remainder.shape[0] % 2 == 0 or whole_x:
        coarse = cycle(restrict(remainder), coarsen(faces), level_index + 1, stride, whole_x)
        field = field + prolong(coarse)
    else:
        field = field + merged_cycle(remainder, faces, level_index, stride)
    for repeat in range(NU):
        field = smooth(field)
    return field


def on_device(right_side, phase):
    cell_beta = jnp.where(phase == 1, 1000.0, 1.0).astype(jnp.bfloat16)
    widened = padded(cell_beta, (("gx", 0), ("gy", 1)), 1).astype(jnp.float32)
    faces = face_table(widened)
    solution = cycle(right_side, faces, 0, 1, False)
    centre = centre_weight(faces)
    applied = centre * solution - weighted(widen(solution, 1), faces)
    return (centre * solution, right_side - applied)


def solution(mesh):
    placed = (P("gx", "gy", None), P("gx", "gy", None))
    return jax.shard_map(
        on_device,
        mesh=mesh,
        in_specs=placed,
        out_specs=(P("gx", "gy", None), P("gx", "gy", None)),
        check_vma=False,
    )
```

profile of v0, /device:TPU:7, one launch (start us, length us, event | category | flops | bytes accessed | tf_op | source)
XLA Modules:
  0.0 415.0 jit_solution(1185598047880235484)
XLA Ops:
  3.7 4.9 %collective-permute-start = (bf16[1,64,128]{2,1,0:T(8,128)(2,1)S(1)}, bf16[1,64,128]{2,1,0:T(8,128)(2,1)S(1)}, u32[]{:S(2)}, u32[]{:S(2)}) collective-permute-start(bf16[1,64,128]{2,1,0:T(8,128)(2,1)S(1)} %get-tuple-element.35), channel_id=1, source_target_pairs={{0,2},{2,4},{4,6},{6,8},{8,10},{10,12},{12,14},{14,16},{16,18},{18... | collective-permute-start | bytes 49160 | tf_op jit(solution)/shard_map/ppermute | solution.py:19
  9.5 3.7 collective-permute-start.3
  22.3 3.0 collective-permute-start.7
  25.2 4.7 %collective-permute-start.4 = (f32[1,64,128]{2,1,0:T(8,128)S(1)}, f32[1,64,128]{2,1,0:T(8,128)S(1)}, u32[]{:S(2)}, u32[]{:S(2)}) collective-permute-start(f32[1,64,128]{2,1,0:T(8,128)S(1)} %get-tuple-element.29), channel_id=1, source_target_pairs={{0,2},{2,4},{4,6},{6,8},{8,10},{10,12},{12,14},{14,16},{16,18},{18... | collective-permute-start | bytes 98312 | tf_op jit(solution)/shard_map/ppermute | solution.py:30
  32.0 2.4 collective-permute-done.31
  34.6 2.3 collective-permute-done.30
  44.4 2.4 collective-permute-start.67
  50.5 2.3 collective-permute-start.66
  53.9 2.4 collective-permute-done.29
  56.9 2.4 collective-permute-done.41
  62.3 15.8 %collective-permute-start.10 = (f32[4,1,128]{2,1,0:T(1,128)S(1)}, f32[4,1,128]{2,1,0:T(1,128)S(1)}, u32[]{:S(2)}, u32[]{:S(2)}) collective-permute-start(f32[4,1,128]{2,1,0:T(1,128)S(1)} %get-tuple-element.28), channel_id=1, source_target_pairs={{1,0},{3,2},{5,4},{7,6},{9,8},{11,10},{13,12},{15,14},{17,16},{19,... | collective-permute-start | bytes 6152 | tf_op jit(solution)/shard_map/ppermute | solution.py:22
  81.3 5.2 %collective-permute-start.8 = (f32[1,64,128]{2,1,0:T(8,128)S(1)}, f32[1,64,128]{2,1,0:T(8,128)S(1)}, u32[]{:S(2)}, u32[]{:S(2)}) collective-permute-start(f32[1,64,128]{2,1,0:T(8,128)S(1)} %get-tuple-element.25), channel_id=1, source_target_pairs={{0,2},{2,4},{4,6},{6,8},{8,10},{10,12},{12,14},{14,16},{16,18},{18... | collective-permute-start | bytes 98312 | tf_op jit(solution)/shard_map/ppermute | solution.py:30
  88.2 4.2 %collective-permute-start.14 = (f32[2,1,64]{2,1,0:T(1,128)S(1)}, f32[2,1,64]{2,1,0:T(1,128)S(1)}, u32[]{:S(2)}, u32[]{:S(2)}) collective-permute-start(f32[2,1,64]{2,1,0:T(1,128)S(1)} %get-tuple-element.52), channel_id=1, source_target_pairs={{1,0},{3,2},{5,4},{7,6},{9,8},{11,10},{13,12},{15,14},{17,16},{19,... | collective-permute-start | bytes 1544 | tf_op jit(solution)/shard_map/ppermute | solution.py:22
  93.7 2.5 collective-permute-start.15
  96.2 5.2 %collective-permute-start.12 = (f32[1,32,64]{2,1,0:T(8,128)S(1)}, f32[1,32,64]{2,1,0:T(8,128)S(1)}, u32[]{:S(2)}, u32[]{:S(2)}) collective-permute-start(f32[1,32,64]{2,1,0:T(8,128)S(1)} %get-tuple-element.49), channel_id=1, source_target_pairs={{0,2},{2,4},{4,6},{6,8},{8,10},{10,12},{12,14},{14,16},{16,18},{18... | collective-permute-start | bytes 24584 | tf_op jit(solution)/shard_map/ppermute | solution.py:30
  102.3 3.9 collective-permute-start.18
  109.4 5.7 %collective-permute-start.16 = (f32[1,32,64]{2,1,0:T(8,128)S(1)}, f32[1,32,64]{2,1,0:T(8,128)S(1)}, u32[]{:S(2)}, u32[]{:S(2)}) collective-permute-start(f32[1,32,64]{2,1,0:T(8,128)S(1)} %get-tuple-element.45), channel_id=1, source_target_pairs={{0,2},{2,4},{4,6},{6,8},{8,10},{10,12},{12,14},{14,16},{16,18},{18... | collective-permute-start | bytes 24584 | tf_op jit(solution)/shard_map/ppermute | solution.py:30
  115.2 2.4 collective-permute-start.65
  118.0 3.9 collective-permute-start.20
  123.8 4.5 %collective-permute-start.23 = (f32[1,1,32]{2,1,0:T(1,128)S(1)}, f32[1,1,32]{2,1,0:T(1,128)S(1)}, u32[]{:S(2)}, u32[]{:S(2)}) collective-permute-start(f32[1,1,32]{2,1,0:T(1,128)S(1)} %get-tuple-element.66), channel_id=1, source_target_pairs={{1,0},{3,2},{5,4},{7,6},{9,8},{11,10},{13,12},{15,14},{17,16},{19,... | collective-permute-start | bytes 392 | tf_op jit(solution)/shard_map/ppermute | solution.py:22
  131.4 5.4 %collective-permute-start.24 = (f32[1,16,32]{2,1,0:T(8,128)S(1)}, f32[1,16,32]{2,1,0:T(8,128)S(1)}, u32[]{:S(2)}, u32[]{:S(2)}) collective-permute-start(f32[1,16,32]{2,1,0:T(8,128)S(1)} %fusion.111), channel_id=1, source_target_pairs={{0,2},{2,4},{4,6},{6,8},{8,10},{10,12},{12,14},{14,16},{16,18},{18... | collective-permute-start | bytes 6152 | tf_op jit(solution)/shard_map/ppermute | solution.py:30
  138.8 2.4 collective-permute-start.27
  144.4 2.5 collective-permute-done.28
  147.1 4.3 %collective-permute-start.32 = (f32[1,8,16]{2,1,0:T(8,128)S(1)}, f32[1,8,16]{2,1,0:T(8,128)S(1)}, u32[]{:S(2)}, u32[]{:S(2)}) collective-permute-start(f32[1,8,16]{2,1,0:T(8,128)S(1)} %bitcast_divide_fusion.2), channel_id=1, source_target_pairs={{0,4},{2,6},{4,8},{6,10},{8,12},{10,14},{12,16},{14,18},{16,20},{1... | collective-permute-start | bytes 1544 | tf_op jit(solution)/shard_map/ppermute | solution.py:30
  153.3 3.2 collective-permute-start.35
  159.7 4.5 %collective-permute-start.36 = (f32[1,8,16]{2,1,0:T(8,128)S(1)}, f32[1,8,16]{2,1,0:T(8,128)S(1)}, u32[]{:S(2)}, u32[]{:S(2)}) collective-permute-start(f32[1,8,16]{2,1,0:T(8,128)S(1)} %fusion.152), channel_id=1, source_target_pairs={{0,4},{2,6},{4,8},{6,10},{8,12},{10,14},{12,16},{14,18},{16,20},{1... | collective-permute-start | bytes 1544 | tf_op jit(solution)/shard_map/ppermute | solution.py:30
  166.2 2.4 collective-permute-start.39
  174.3 3.4 collective-permute-start.44
  180.3 3.3 collective-permute-start.47
  184.7 4.3 %collective-permute-start.48 = (f32[1,4,8]{1,2,0:T(8,128)S(1)}, f32[1,4,8]{1,2,0:T(8,128)S(1)}, u32[]{:S(2)}, u32[]{:S(2)}) collective-permute-start(f32[1,4,8]{1,2,0:T(8,128)S(1)} %fusion.190), channel_id=1, source_target_pairs={{0,8},{2,10},{4,12},{6,14},{8,16},{10,18},{12,20},{14,22},{16,24},... | collective-permute-start | bytes 392 | tf_op jit(solution)/shard_map/ppermute | solution.py:30
  191.6 3.0 collective-permute-start.51
  200.3 4.9 %collective-permute-start.56 = (f32[1,2,4]{2,1,0:T(2,128)S(1)}, f32[1,2,4]{2,1,0:T(2,128)S(1)}, u32[]{:S(2)}, u32[]{:S(2)}) collective-permute-start(f32[1,2,4]{2,1,0:T(2,128)S(1)} %get-tuple-element.9), channel_id=1, source_target_pairs={{0,16},{2,18},{4,20},{6,22},{8,24},{10,26},{12,28},{14,30},{1,17},... | collective-permute-start | bytes 104 | tf_op jit(solution)/shard_map/ppermute | solution.py:30
  206.5 3.7 collective-permute-start.59
  212.4 4.9 %collective-permute-start.60 = (f32[1,2,4]{2,1,0:T(2,128)S(1)}, f32[1,2,4]{2,1,0:T(2,128)S(1)}, u32[]{:S(2)}, u32[]{:S(2)}) collective-permute-start(f32[1,2,4]{2,1,0:T(2,128)S(1)} %fusion.255), channel_id=1, source_target_pairs={{0,16},{2,18},{4,20},{6,22},{8,24},{10,26},{12,28},{14,30},{1,17},... | collective-permute-start | bytes 104 | tf_op jit(solution)/shard_map/ppermute | solution.py:30
  218.6 3.0 collective-permute-start.63
  222.6 3.3 collective-permute-done.64
  226.2 3.4 collective-permute-start.70
  255.0 4.9 %collective-permute-start.83 = (f32[1,2,4]{2,1,0:T(2,128)S(1)}, f32[1,2,4]{2,1,0:T(2,128)S(1)}, u32[]{:S(2)}, u32[]{:S(2)}) collective-permute-start(f32[1,2,4]{2,1,0:T(2,128)S(1)} %broadcast_add_fusion.1), channel_id=1, source_target_pairs={{0,16},{2,18},{4,20},{6,22},{8,24},{10,26},{12,28},{14,30},{1,17},... | collective-permute-start | bytes 104 | tf_op jit(solution)/shard_map/ppermute | solution.py:30
  261.2 3.2 collective-permute-start.86
  266.5 4.9 %collective-permute-start.87 = (f32[1,2,4]{2,1,0:T(2,128)S(1)}, f32[1,2,4]{2,1,0:T(2,128)S(1)}, u32[]{:S(2)}, u32[]{:S(2)}) collective-permute-start(f32[1,2,4]{2,1,0:T(2,128)S(1)} %fusion.254), channel_id=1, source_target_pairs={{0,16},{2,18},{4,20},{6,22},{8,24},{10,26},{12,28},{14,30},{1,17},... | collective-permute-start | bytes 104 | tf_op jit(solution)/shard_map/ppermute | solution.py:30
  272.7 3.0 collective-permute-start.90
  276.7 3.6 collective-permute-start.91
  283.0 3.0 collective-permute-start.94
  287.0 4.0 collective-permute-start.95
  293.7 3.0 collective-permute-start.98
  297.9 5.3 %collective-permute-start.99 = (f32[1,8,16]{2,1,0:T(8,128)S(1)}, f32[1,8,16]{2,1,0:T(8,128)S(1)}, u32[]{:S(2)}, u32[]{:S(2)}) collective-permute-start(f32[1,8,16]{2,1,0:T(8,128)S(1)} %add.950), channel_id=1, source_target_pairs={{0,4},{2,6},{4,8},{6,10},{8,12},{10,14},{12,16},{14,18},{16,20},{1... | collective-permute-start | bytes 1544 | tf_op jit(solution)/shard_map/ppermute | solution.py:30
  305.2 2.5 collective-permute-start.102
  312.8 4.5 %collective-permute-start.103 = (f32[1,8,16]{2,1,0:T(8,128)S(1)}, f32[1,8,16]{2,1,0:T(8,128)S(1)}, u32[]{:S(2)}, u32[]{:S(2)}) collective-permute-start(f32[1,8,16]{2,1,0:T(8,128)S(1)} %fusion.169), channel_id=1, source_target_pairs={{0,4},{2,6},{4,8},{6,10},{8,12},{10,14},{12,16},{14,18},{16,20},{1... | collective-permute-start | bytes 1544 | tf_op jit(solution)/shard_map/ppermute | solution.py:30
  317.4 2.4 collective-permute-start.106
  323.1 5.1 %collective-permute-start.107 = (f32[1,16,32]{2,1,0:T(8,128)S(1)}, f32[1,16,32]{2,1,0:T(8,128)S(1)}, u32[]{:S(2)}, u32[]{:S(2)}) collective-permute-start(f32[1,16,32]{2,1,0:T(8,128)S(1)} %add.964), channel_id=1, source_target_pairs={{0,2},{2,4},{4,6},{6,8},{8,10},{10,12},{12,14},{14,16},{16,18},{18... | collective-permute-start | bytes 6152 | tf_op jit(solution)/shard_map/ppermute | solution.py:30
  330.1 2.4 collective-permute-start.110
  335.6 3.1 collective-permute-start.112
  338.7 4.3 %collective-permute-start.111 = (f32[1,16,32]{2,1,0:T(8,128)S(1)}, f32[1,16,32]{2,1,0:T(8,128)S(1)}, u32[]{:S(2)}, u32[]{:S(2)}) collective-permute-start(f32[1,16,32]{2,1,0:T(8,128)S(1)} %fusion.128), channel_id=1, source_target_pairs={{0,2},{2,4},{4,6},{6,8},{8,10},{10,12},{12,14},{14,16},{16,18},{18... | collective-permute-start | bytes 6152 | tf_op jit(solution)/shard_map/ppermute | solution.py:30
  343.0 2.6 collective-permute-start.114
  350.9 5.2 %collective-permute-start.115 = (f32[1,32,64]{2,1,0:T(8,128)S(1)}, f32[1,32,64]{2,1,0:T(8,128)S(1)}, u32[]{:S(2)}, u32[]{:S(2)}) collective-permute-start(f32[1,32,64]{2,1,0:T(8,128)S(1)} %get-tuple-element.41), channel_id=1, source_target_pairs={{0,2},{2,4},{4,6},{6,8},{8,10},{10,12},{12,14},{14,16},{16,18},{18... | collective-permute-start | bytes 24584 | tf_op jit(solution)/shard_map/ppermute | solution.py:30
  356.1 2.6 collective-permute-start.117
  363.8 5.2 %collective-permute-start.119 = (f32[1,32,64]{2,1,0:T(8,128)S(1)}, f32[1,32,64]{2,1,0:T(8,128)S(1)}, u32[]{:S(2)}, u32[]{:S(2)}) collective-permute-start(f32[1,32,64]{2,1,0:T(8,128)S(1)} %get-tuple-element.37), channel_id=1, source_target_pairs={{0,2},{2,4},{4,6},{6,8},{8,10},{10,12},{12,14},{14,16},{16,18},{18... | collective-permute-start | bytes 24584 | tf_op jit(solution)/shard_map/ppermute | solution.py:30
  369.0 2.6 collective-permute-start.121
  377.2 5.2 %collective-permute-start.123 = (f32[1,64,128]{2,1,0:T(8,128)S(1)}, f32[1,64,128]{2,1,0:T(8,128)S(1)}, u32[]{:S(2)}, u32[]{:S(2)}) collective-permute-start(f32[1,64,128]{2,1,0:T(8,128)S(1)} %get-tuple-element.21), channel_id=1, source_target_pairs={{0,2},{2,4},{4,6},{6,8},{8,10},{10,12},{12,14},{14,16},{16,18},{18... | collective-permute-start | bytes 98312 | tf_op jit(solution)/shard_map/ppermute | solution.py:30
  382.3 2.6 collective-permute-start.125
  390.2 5.2 %collective-permute-start.127 = (f32[1,64,128]{2,1,0:T(8,128)S(1)}, f32[1,64,128]{2,1,0:T(8,128)S(1)}, u32[]{:S(2)}, u32[]{:S(2)}) collective-permute-start(f32[1,64,128]{2,1,0:T(8,128)S(1)} %get-tuple-element.17), channel_id=1, source_target_pairs={{0,2},{2,4},{4,6},{6,8},{8,10},{10,12},{12,14},{14,16},{16,18},{18... | collective-permute-start | bytes 98312 | tf_op jit(solution)/shard_map/ppermute | solution.py:30
  395.4 2.6 collective-permute-start.129
  403.3 5.2 %collective-permute-start.131 = (f32[1,64,128]{2,1,0:T(8,128)S(1)}, f32[1,64,128]{2,1,0:T(8,128)S(1)}, u32[]{:S(2)}, u32[]{:S(2)}) collective-permute-start(f32[1,64,128]{2,1,0:T(8,128)S(1)} %get-tuple-element.13), channel_id=1, source_target_pairs={{0,2},{2,4},{4,6},{6,8},{8,10},{10,12},{12,14},{14,16},{16,18},{18... | collective-permute-start | bytes 98312 | tf_op jit(solution)/shard_map/ppermute | solution.py:30
  408.4 2.6 collective-permute-start.133
  (475 shorter events, 166.1 us)
Async XLA Ops:
  1.6 7.1 %collective-permute-start.1 = (bf16[1,64,128]{2,1,0:T(8,128)(2,1)S(1)}, bf16[1,64,128]{2,1,0:T(8,128)(2,1)S(1)}, u32[]{:S(2)}, u32[]{:S(2)}) collective-permute-start(bf16[1,64,128]{2,1,0:T(8,128)(2,1)S(1)} %get-tuple-element.36), channel_id=1, source_target_pairs={{2,0},{4,2},{6,4},{8,6},{10,8},{12,10},{14,12},{16,14},{18,16},{20... | collective-permute-start | bytes 49160 | tf_op jit(solution)/shard_map/ppermute | solution.py:22
  3.7 5.8 %collective-permute-start = (bf16[1,64,128]{2,1,0:T(8,128)(2,1)S(1)}, bf16[1,64,128]{2,1,0:T(8,128)(2,1)S(1)}, u32[]{:S(2)}, u32[]{:S(2)}) collective-permute-start(bf16[1,64,128]{2,1,0:T(8,128)(2,1)S(1)} %get-tuple-element.35), channel_id=1, source_target_pairs={{0,2},{2,4},{4,6},{6,8},{8,10},{10,12},{12,14},{14,16},{16,18},{18... | collective-permute-start | bytes 49160 | tf_op jit(solution)/shard_map/ppermute | solution.py:19
  9.5 5.1 %collective-permute-start.3 = (bf16[6,1,128]{2,1,0:T(2,128)(2,1)S(1)}, bf16[6,1,128]{2,1,0:T(2,128)(2,1)S(1)}, u32[]{:S(2)}, u32[]{:S(2)}) collective-permute-start(bf16[6,1,128]{2,1,0:T(2,128)(2,1)S(1)} %get-tuple-element.34), channel_id=1, source_target_pairs={{1,0},{3,2},{5,4},{7,6},{9,8},{11,10},{13,12},{15,14},{17,16},{19,... | collective-permute-start | bytes 4616 | tf_op jit(solution)/shard_map/ppermute | solution.py:22
  18.9 43.1 %collective-permute-start.6 = (f32[4,1,128]{2,1,0:T(1,128)S(1)}, f32[4,1,128]{2,1,0:T(1,128)S(1)}, u32[]{:S(2)}, u32[]{:S(2)}) collective-permute-start(f32[4,1,128]{2,1,0:T(1,128)S(1)} %get-tuple-element.32), channel_id=1, source_target_pairs={{1,0},{3,2},{5,4},{7,6},{9,8},{11,10},{13,12},{15,14},{17,16},{19,... | collective-permute-start | bytes 6152 | tf_op jit(solution)/shard_map/ppermute | solution.py:22
  21.0 41.0 %collective-permute-start.5 = (f32[4,1,128]{2,1,0:T(1,128)S(1)}, f32[4,1,128]{2,1,0:T(1,128)S(1)}, u32[]{:S(2)}, u32[]{:S(2)}) collective-permute-start(f32[4,1,128]{2,1,0:T(1,128)S(1)} %get-tuple-element.31), channel_id=1, source_target_pairs={{0,1},{2,3},{4,5},{6,7},{8,9},{10,11},{12,13},{14,15},{16,17},{18,... | collective-permute-start | bytes 6152 | tf_op jit(solution)/shard_map/ppermute | solution.py:19
  22.3 39.7 %collective-permute-start.7 = (f32[1,64,128]{2,1,0:T(8,128)S(1)}, f32[1,64,128]{2,1,0:T(8,128)S(1)}, u32[]{:S(2)}, u32[]{:S(2)}) collective-permute-start(f32[1,64,128]{2,1,0:T(8,128)S(1)} %get-tuple-element.30), channel_id=1, source_target_pairs={{2,0},{4,2},{6,4},{8,6},{10,8},{12,10},{14,12},{16,14},{18,16},{20... | collective-permute-start | bytes 98312 | tf_op jit(solution)/shard_map/ppermute | solution.py:30
  25.2 36.8 %collective-permute-start.4 = (f32[1,64,128]{2,1,0:T(8,128)S(1)}, f32[1,64,128]{2,1,0:T(8,128)S(1)}, u32[]{:S(2)}, u32[]{:S(2)}) collective-permute-start(f32[1,64,128]{2,1,0:T(8,128)S(1)} %get-tuple-element.29), channel_id=1, source_target_pairs={{0,2},{2,4},{4,6},{6,8},{8,10},{10,12},{12,14},{14,16},{16,18},{18... | collective-permute-start | bytes 98312 | tf_op jit(solution)/shard_map/ppermute | solution.py:30
  62.3 24.2 %collective-permute-start.10 = (f32[4,1,128]{2,1,0:T(1,128)S(1)}, f32[4,1,128]{2,1,0:T(1,128)S(1)}, u32[]{:S(2)}, u32[]{:S(2)}) collective-permute-start(f32[4,1,128]{2,1,0:T(1,128)S(1)} %get-tuple-element.28), channel_id=1, source_target_pairs={{1,0},{3,2},{5,4},{7,6},{9,8},{11,10},{13,12},{15,14},{17,16},{19,... | collective-permute-start | bytes 6152 | tf_op jit(solution)/shard_map/ppermute | solution.py:22
  78.1 8.4 %collective-permute-start.9 = (f32[4,1,128]{2,1,0:T(1,128)S(1)}, f32[4,1,128]{2,1,0:T(1,128)S(1)}, u32[]{:S(2)}, u32[]{:S(2)}) collective-permute-start(f32[4,1,128]{2,1,0:T(1,128)S(1)} %get-tuple-element.27), channel_id=1, source_target_pairs={{0,1},{2,3},{4,5},{6,7},{8,9},{10,11},{12,13},{14,15},{16,17},{18,... | collective-permute-start | bytes 6152 | tf_op jit(solution)/shard_map/ppermute | solution.py:19
  79.4 7.1 %collective-permute-start.11 = (f32[1,64,128]{2,1,0:T(8,128)S(1)}, f32[1,64,128]{2,1,0:T(8,128)S(1)}, u32[]{:S(2)}, u32[]{:S(2)}) collective-permute-start(f32[1,64,128]{2,1,0:T(8,128)S(1)} %get-tuple-element.26), channel_id=1, source_target_pairs={{2,0},{4,2},{6,4},{8,6},{10,8},{12,10},{14,12},{16,14},{18,16},{20... | collective-permute-start | bytes 98312 | tf_op jit(solution)/shard_map/ppermute | solution.py:30
  81.3 6.2 %collective-permute-start.8 = (f32[1,64,128]{2,1,0:T(8,128)S(1)}, f32[1,64,128]{2,1,0:T(8,128)S(1)}, u32[]{:S(2)}, u32[]{:S(2)}) collective-permute-start(f32[1,64,128]{2,1,0:T(8,128)S(1)} %get-tuple-element.25), channel_id=1, source_target_pairs={{0,2},{2,4},{4,6},{6,8},{8,10},{10,12},{12,14},{14,16},{16,18},{18... | collective-permute-start | bytes 98312 | tf_op jit(solution)/shard_map/ppermute | solution.py:30
  88.2 13.4 %collective-permute-start.14 = (f32[2,1,64]{2,1,0:T(1,128)S(1)}, f32[2,1,64]{2,1,0:T(1,128)S(1)}, u32[]{:S(2)}, u32[]{:S(2)}) collective-permute-start(f32[2,1,64]{2,1,0:T(1,128)S(1)} %get-tuple-element.52), channel_id=1, source_target_pairs={{1,0},{3,2},{5,4},{7,6},{9,8},{11,10},{13,12},{15,14},{17,16},{19,... | collective-permute-start | bytes 1544 | tf_op jit(solution)/shard_map/ppermute | solution.py:22
  92.4 9.3 %collective-permute-start.13 = (f32[2,1,64]{2,1,0:T(1,128)S(1)}, f32[2,1,64]{2,1,0:T(1,128)S(1)}, u32[]{:S(2)}, u32[]{:S(2)}) collective-permute-start(f32[2,1,64]{2,1,0:T(1,128)S(1)} %get-tuple-element.51), channel_id=1, source_target_pairs={{0,1},{2,3},{4,5},{6,7},{8,9},{10,11},{12,13},{14,15},{16,17},{18,... | collective-permute-start | bytes 1544 | tf_op jit(solution)/shard_map/ppermute | solution.py:19
  93.7 8.0 %collective-permute-start.15 = (f32[1,32,64]{2,1,0:T(8,128)S(1)}, f32[1,32,64]{2,1,0:T(8,128)S(1)}, u32[]{:S(2)}, u32[]{:S(2)}) collective-permute-start(f32[1,32,64]{2,1,0:T(8,128)S(1)} %get-tuple-element.50), channel_id=1, source_target_pairs={{2,0},{4,2},{6,4},{8,6},{10,8},{12,10},{14,12},{16,14},{18,16},{20... | collective-permute-start | bytes 24584 | tf_op jit(solution)/shard_map/ppermute | solution.py:30
  96.2 6.0 %collective-permute-start.12 = (f32[1,32,64]{2,1,0:T(8,128)S(1)}, f32[1,32,64]{2,1,0:T(8,128)S(1)}, u32[]{:S(2)}, u32[]{:S(2)}) collective-permute-start(f32[1,32,64]{2,1,0:T(8,128)S(1)} %get-tuple-element.49), channel_id=1, source_target_pairs={{0,2},{2,4},{4,6},{6,8},{8,10},{10,12},{12,14},{14,16},{16,18},{18... | collective-permute-start | bytes 24584 | tf_op jit(solution)/shard_map/ppermute | solution.py:30
  102.3 15.2 %collective-permute-start.18 = (f32[2,1,64]{2,1,0:T(1,128)S(1)}, f32[2,1,64]{2,1,0:T(1,128)S(1)}, u32[]{:S(2)}, u32[]{:S(2)}) collective-permute-start(f32[2,1,64]{2,1,0:T(1,128)S(1)} %get-tuple-element.48), channel_id=1, source_target_pairs={{1,0},{3,2},{5,4},{7,6},{9,8},{11,10},{13,12},{15,14},{17,16},{19,... | collective-permute-start | bytes 1544 | tf_op jit(solution)/shard_map/ppermute | solution.py:22
  106.2 11.3 %collective-permute-start.17 = (f32[2,1,64]{2,1,0:T(1,128)S(1)}, f32[2,1,64]{2,1,0:T(1,128)S(1)}, u32[]{:S(2)}, u32[]{:S(2)}) collective-permute-start(f32[2,1,64]{2,1,0:T(1,128)S(1)} %get-tuple-element.47), channel_id=1, source_target_pairs={{0,1},{2,3},{4,5},{6,7},{8,9},{10,11},{12,13},{14,15},{16,17},{18,... | collective-permute-start | bytes 1544 | tf_op jit(solution)/shard_map/ppermute | solution.py:19
  107.5 10.1 %collective-permute-start.19 = (f32[1,32,64]{2,1,0:T(8,128)S(1)}, f32[1,32,64]{2,1,0:T(8,128)S(1)}, u32[]{:S(2)}, u32[]{:S(2)}) collective-permute-start(f32[1,32,64]{2,1,0:T(8,128)S(1)} %get-tuple-element.46), channel_id=1, source_target_pairs={{2,0},{4,2},{6,4},{8,6},{10,8},{12,10},{14,12},{16,14},{18,16},{20... | collective-permute-start | bytes 24584 | tf_op jit(solution)/shard_map/ppermute | solution.py:30
  109.4 8.1 %collective-permute-start.16 = (f32[1,32,64]{2,1,0:T(8,128)S(1)}, f32[1,32,64]{2,1,0:T(8,128)S(1)}, u32[]{:S(2)}, u32[]{:S(2)}) collective-permute-start(f32[1,32,64]{2,1,0:T(8,128)S(1)} %get-tuple-element.45), channel_id=1, source_target_pairs={{0,2},{2,4},{4,6},{6,8},{8,10},{10,12},{12,14},{14,16},{16,18},{18... | collective-permute-start | bytes 24584 | tf_op jit(solution)/shard_map/ppermute | solution.py:30
  115.2 14.4 %collective-permute-start.65 = (bf16[2,2,4]{2,1,0:T(2,128)(2,1)S(1)}, bf16[2,2,4]{2,1,0:T(2,128)(2,1)S(1)}, u32[]{:S(2)}, u32[]{:S(2)}) collective-permute-start(bf16[2,2,4]{2,1,0:T(2,128)(2,1)S(1)} %multiply_convert_fusion.12), channel_id=1, source_target_pairs={{0,16},{2,18},{4,20},{6,22},{8,24},{10,26},{12,28},{14,30},{16,0},... | collective-permute-start | bytes 104 | tf_op jit(solution)/shard_map/ppermute | solution.py:36
  118.0 13.3 %collective-permute-start.20 = (f32[1,16,32]{2,1,0:T(8,128)S(1)}, f32[1,16,32]{2,1,0:T(8,128)S(1)}, u32[]{:S(2)}, u32[]{:S(2)}) collective-permute-start(f32[1,16,32]{2,1,0:T(8,128)S(1)} %bitcast_divide_fusion), channel_id=1, source_target_pairs={{0,2},{2,4},{4,6},{6,8},{8,10},{10,12},{12,14},{14,16},{16,18},{18... | collective-permute-start | bytes 6152 | tf_op jit(solution)/shard_map/ppermute | solution.py:30
  121.9 9.5 %collective-permute-start.21 = (f32[1,16,32]{2,1,0:T(8,128)S(1)}, f32[1,16,32]{2,1,0:T(8,128)S(1)}, u32[]{:S(2)}, u32[]{:S(2)}) collective-permute-start(f32[1,16,32]{2,1,0:T(8,128)S(1)} %bitcast_divide_fusion), channel_id=1, source_target_pairs={{2,0},{4,2},{6,4},{8,6},{10,8},{12,10},{14,12},{16,14},{18,16},{20... | collective-permute-start | bytes 6152 | tf_op jit(solution)/shard_map/ppermute | solution.py:30
  123.8 5.8 %collective-permute-start.23 = (f32[1,1,32]{2,1,0:T(1,128)S(1)}, f32[1,1,32]{2,1,0:T(1,128)S(1)}, u32[]{:S(2)}, u32[]{:S(2)}) collective-permute-start(f32[1,1,32]{2,1,0:T(1,128)S(1)} %get-tuple-element.66), channel_id=1, source_target_pairs={{1,0},{3,2},{5,4},{7,6},{9,8},{11,10},{13,12},{15,14},{17,16},{19,... | collective-permute-start | bytes 392 | tf_op jit(solution)/shard_map/ppermute | solution.py:22
  131.4 12.8 %collective-permute-start.24 = (f32[1,16,32]{2,1,0:T(8,128)S(1)}, f32[1,16,32]{2,1,0:T(8,128)S(1)}, u32[]{:S(2)}, u32[]{:S(2)}) collective-permute-start(f32[1,16,32]{2,1,0:T(8,128)S(1)} %fusion.111), channel_id=1, source_target_pairs={{0,2},{2,4},{4,6},{6,8},{8,10},{10,12},{12,14},{14,16},{16,18},{18... | collective-permute-start | bytes 6152 | tf_op jit(solution)/shard_map/ppermute | solution.py:30
  136.8 7.4 %collective-permute-start.25 = (f32[1,16,32]{2,1,0:T(8,128)S(1)}, f32[1,16,32]{2,1,0:T(8,128)S(1)}, u32[]{:S(2)}, u32[]{:S(2)}) collective-permute-start(f32[1,16,32]{2,1,0:T(8,128)S(1)} %fusion.111), channel_id=1, source_target_pairs={{2,0},{4,2},{6,4},{8,6},{10,8},{12,10},{14,12},{16,14},{18,16},{20... | collective-permute-start | bytes 6152 | tf_op jit(solution)/shard_map/ppermute | solution.py:30
  147.1 12.5 %collective-permute-start.32 = (f32[1,8,16]{2,1,0:T(8,128)S(1)}, f32[1,8,16]{2,1,0:T(8,128)S(1)}, u32[]{:S(2)}, u32[]{:S(2)}) collective-permute-start(f32[1,8,16]{2,1,0:T(8,128)S(1)} %bitcast_divide_fusion.2), channel_id=1, source_target_pairs={{0,4},{2,6},{4,8},{6,10},{8,12},{10,14},{12,16},{14,18},{16,20},{1... | collective-permute-start | bytes 1544 | tf_op jit(solution)/shard_map/ppermute | solution.py:30
  151.4 8.2 %collective-permute-start.33 = (f32[1,8,16]{2,1,0:T(8,128)S(1)}, f32[1,8,16]{2,1,0:T(8,128)S(1)}, u32[]{:S(2)}, u32[]{:S(2)}) collective-permute-start(f32[1,8,16]{2,1,0:T(8,128)S(1)} %bitcast_divide_fusion.2), channel_id=1, source_target_pairs={{4,0},{6,2},{8,4},{10,6},{12,8},{14,10},{16,12},{18,14},{20,16},{2... | collective-permute-start | bytes 1544 | tf_op jit(solution)/shard_map/ppermute | solution.py:30
  159.7 11.9 %collective-permute-start.36 = (f32[1,8,16]{2,1,0:T(8,128)S(1)}, f32[1,8,16]{2,1,0:T(8,128)S(1)}, u32[]{:S(2)}, u32[]{:S(2)}) collective-permute-start(f32[1,8,16]{2,1,0:T(8,128)S(1)} %fusion.152), channel_id=1, source_target_pairs={{0,4},{2,6},{4,8},{6,10},{8,12},{10,14},{12,16},{14,18},{16,20},{1... | collective-permute-start | bytes 1544 | tf_op jit(solution)/shard_map/ppermute | solution.py:30
  164.2 7.4 %collective-permute-start.37 = (f32[1,8,16]{2,1,0:T(8,128)S(1)}, f32[1,8,16]{2,1,0:T(8,128)S(1)}, u32[]{:S(2)}, u32[]{:S(2)}) collective-permute-start(f32[1,8,16]{2,1,0:T(8,128)S(1)} %fusion.152), channel_id=1, source_target_pairs={{4,0},{6,2},{8,4},{10,6},{12,8},{14,10},{16,12},{18,14},{20,16},{2... | collective-permute-start | bytes 1544 | tf_op jit(solution)/shard_map/ppermute | solution.py:30
  174.3 10.3 %collective-permute-start.44 = (f32[1,4,8]{1,2,0:T(8,128)S(1)}, f32[1,4,8]{1,2,0:T(8,128)S(1)}, u32[]{:S(2)}, u32[]{:S(2)}) collective-permute-start(f32[1,4,8]{1,2,0:T(8,128)S(1)} %bitcast_divide_fusion.1), channel_id=1, source_target_pairs={{0,8},{2,10},{4,12},{6,14},{8,16},{10,18},{12,20},{14,22},{16,24},... | collective-permute-start | bytes 392 | tf_op jit(solution)/shard_map/ppermute | solution.py:30
  177.7 6.9 %collective-permute-start.45 = (f32[1,4,8]{1,2,0:T(8,128)S(1)}, f32[1,4,8]{1,2,0:T(8,128)S(1)}, u32[]{:S(2)}, u32[]{:S(2)}) collective-permute-start(f32[1,4,8]{1,2,0:T(8,128)S(1)} %bitcast_divide_fusion.1), channel_id=1, source_target_pairs={{8,0},{10,2},{12,4},{14,6},{16,8},{18,10},{20,12},{22,14},{24,16},... | collective-permute-start | bytes 392 | tf_op jit(solution)/shard_map/ppermute | solution.py:30
  184.7 10.8 %collective-permute-start.48 = (f32[1,4,8]{1,2,0:T(8,128)S(1)}, f32[1,4,8]{1,2,0:T(8,128)S(1)}, u32[]{:S(2)}, u32[]{:S(2)}) collective-permute-start(f32[1,4,8]{1,2,0:T(8,128)S(1)} %fusion.190), channel_id=1, source_target_pairs={{0,8},{2,10},{4,12},{6,14},{8,16},{10,18},{12,20},{14,22},{16,24},... | collective-permute-start | bytes 392 | tf_op jit(solution)/shard_map/ppermute | solution.py:30
  188.9 6.6 %collective-permute-start.49 = (f32[1,4,8]{1,2,0:T(8,128)S(1)}, f32[1,4,8]{1,2,0:T(8,128)S(1)}, u32[]{:S(2)}, u32[]{:S(2)}) collective-permute-start(f32[1,4,8]{1,2,0:T(8,128)S(1)} %fusion.190), channel_id=1, source_target_pairs={{8,0},{10,2},{12,4},{14,6},{16,8},{18,10},{20,12},{22,14},{24,16},... | collective-permute-start | bytes 392 | tf_op jit(solution)/shard_map/ppermute | solution.py:30
  199.0 12.0 %collective-permute-start.57 = (f32[1,2,4]{2,1,0:T(2,128)S(1)}, f32[1,2,4]{2,1,0:T(2,128)S(1)}, u32[]{:S(2)}, u32[]{:S(2)}) collective-permute-start(f32[1,2,4]{2,1,0:T(2,128)S(1)} %get-tuple-element.9), channel_id=1, source_target_pairs={{16,0},{18,2},{20,4},{22,6},{24,8},{26,10},{28,12},{30,14},{17,1},... | collective-permute-start | bytes 104 | tf_op jit(solution)/shard_map/ppermute | solution.py:30
  200.3 10.7 %collective-permute-start.56 = (f32[1,2,4]{2,1,0:T(2,128)S(1)}, f32[1,2,4]{2,1,0:T(2,128)S(1)}, u32[]{:S(2)}, u32[]{:S(2)}) collective-permute-start(f32[1,2,4]{2,1,0:T(2,128)S(1)} %get-tuple-element.9), channel_id=1, source_target_pairs={{0,16},{2,18},{4,20},{6,22},{8,24},{10,26},{12,28},{14,30},{1,17},... | collective-permute-start | bytes 104 | tf_op jit(solution)/shard_map/ppermute | solution.py:30
  211.1 11.3 %collective-permute-start.61 = (f32[1,2,4]{2,1,0:T(2,128)S(1)}, f32[1,2,4]{2,1,0:T(2,128)S(1)}, u32[]{:S(2)}, u32[]{:S(2)}) collective-permute-start(f32[1,2,4]{2,1,0:T(2,128)S(1)} %fusion.255), channel_id=1, source_target_pairs={{16,0},{18,2},{20,4},{22,6},{24,8},{26,10},{28,12},{30,14},{17,1},... | collective-permute-start | bytes 104 | tf_op jit(solution)/shard_map/ppermute | solution.py:30
  212.4 10.0 %collective-permute-start.60 = (f32[1,2,4]{2,1,0:T(2,128)S(1)}, f32[1,2,4]{2,1,0:T(2,128)S(1)}, u32[]{:S(2)}, u32[]{:S(2)}) collective-permute-start(f32[1,2,4]{2,1,0:T(2,128)S(1)} %fusion.255), channel_id=1, source_target_pairs={{0,16},{2,18},{4,20},{6,22},{8,24},{10,26},{12,28},{14,30},{1,17},... | collective-permute-start | bytes 104 | tf_op jit(solution)/shard_map/ppermute | solution.py:30
  226.2 5.4 %collective-permute-start.70 = (f32[1,1,2]{2,1,0:T(1,128)S(1)}, f32[1,1,2]{2,1,0:T(1,128)S(1)}, u32[]{:S(2)}, u32[]{:S(2)}) collective-permute-start(f32[1,1,2]{2,1,0:T(1,128)S(1)} %get-tuple-element.6), channel_id=1, source_target_pairs={{1,0},{3,2},{5,4},{7,6},{9,8},{11,10},{13,12},{15,14},{17,16},{19,... | collective-permute-start | bytes 32 | tf_op jit(solution)/shard_map/ppermute | solution.py:22
  253.8 11.3 %collective-permute-start.84 = (f32[1,2,4]{2,1,0:T(2,128)S(1)}, f32[1,2,4]{2,1,0:T(2,128)S(1)}, u32[]{:S(2)}, u32[]{:S(2)}) collective-permute-start(f32[1,2,4]{2,1,0:T(2,128)S(1)} %broadcast_add_fusion.1), channel_id=1, source_target_pairs={{16,0},{18,2},{20,4},{22,6},{24,8},{26,10},{28,12},{30,14},{17,1},... | collective-permute-start | bytes 104 | tf_op jit(solution)/shard_map/ppermute | solution.py:30
  255.0 10.0 %collective-permute-start.83 = (f32[1,2,4]{2,1,0:T(2,128)S(1)}, f32[1,2,4]{2,1,0:T(2,128)S(1)}, u32[]{:S(2)}, u32[]{:S(2)}) collective-permute-start(f32[1,2,4]{2,1,0:T(2,128)S(1)} %broadcast_add_fusion.1), channel_id=1, source_target_pairs={{0,16},{2,18},{4,20},{6,22},{8,24},{10,26},{12,28},{14,30},{1,17},... | collective-permute-start | bytes 104 | tf_op jit(solution)/shard_map/ppermute | solution.py:30
  265.2 11.3 %collective-permute-start.88 = (f32[1,2,4]{2,1,0:T(2,128)S(1)}, f32[1,2,4]{2,1,0:T(2,128)S(1)}, u32[]{:S(2)}, u32[]{:S(2)}) collective-permute-start(f32[1,2,4]{2,1,0:T(2,128)S(1)} %fusion.254), channel_id=1, source_target_pairs={{16,0},{18,2},{20,4},{22,6},{24,8},{26,10},{28,12},{30,14},{17,1},... | collective-permute-start | bytes 104 | tf_op jit(solution)/shard_map/ppermute | solution.py:30
  266.5 10.0 %collective-permute-start.87 = (f32[1,2,4]{2,1,0:T(2,128)S(1)}, f32[1,2,4]{2,1,0:T(2,128)S(1)}, u32[]{:S(2)}, u32[]{:S(2)}) collective-permute-start(f32[1,2,4]{2,1,0:T(2,128)S(1)} %fusion.254), channel_id=1, source_target_pairs={{0,16},{2,18},{4,20},{6,22},{8,24},{10,26},{12,28},{14,30},{1,17},... | collective-permute-start | bytes 104 | tf_op jit(solution)/shard_map/ppermute | solution.py:30
  276.7 10.2 %collective-permute-start.91 = (f32[1,4,8]{1,2,0:T(8,128)S(1)}, f32[1,4,8]{1,2,0:T(8,128)S(1)}, u32[]{:S(2)}, u32[]{:S(2)}) collective-permute-start(f32[1,4,8]{1,2,0:T(8,128)S(1)} %add.936), channel_id=1, source_target_pairs={{0,8},{2,10},{4,12},{6,14},{8,16},{10,18},{12,20},{14,22},{16,24},... | collective-permute-start | bytes 392 | tf_op jit(solution)/shard_map/ppermute | solution.py:30
  280.4 6.6 %collective-permute-start.92 = (f32[1,4,8]{1,2,0:T(8,128)S(1)}, f32[1,4,8]{1,2,0:T(8,128)S(1)}, u32[]{:S(2)}, u32[]{:S(2)}) collective-permute-start(f32[1,4,8]{1,2,0:T(8,128)S(1)} %add.936), channel_id=1, source_target_pairs={{8,0},{10,2},{12,4},{14,6},{16,8},{18,10},{20,12},{22,14},{24,16},... | collective-permute-start | bytes 392 | tf_op jit(solution)/shard_map/ppermute | solution.py:30
  287.0 10.6 %collective-permute-start.95 = (f32[1,4,8]{1,2,0:T(8,128)S(1)}, f32[1,4,8]{1,2,0:T(8,128)S(1)}, u32[]{:S(2)}, u32[]{:S(2)}) collective-permute-start(f32[1,4,8]{1,2,0:T(8,128)S(1)} %fusion.207), channel_id=1, source_target_pairs={{0,8},{2,10},{4,12},{6,14},{8,16},{10,18},{12,20},{14,22},{16,24},... | collective-permute-start | bytes 392 | tf_op jit(solution)/shard_map/ppermute | solution.py:30
  291.0 6.6 %collective-permute-start.96 = (f32[1,4,8]{1,2,0:T(8,128)S(1)}, f32[1,4,8]{1,2,0:T(8,128)S(1)}, u32[]{:S(2)}, u32[]{:S(2)}) collective-permute-start(f32[1,4,8]{1,2,0:T(8,128)S(1)} %fusion.207), channel_id=1, source_target_pairs={{8,0},{10,2},{12,4},{14,6},{16,8},{18,10},{20,12},{22,14},{24,16},... | collective-permute-start | bytes 392 | tf_op jit(solution)/shard_map/ppermute | solution.py:30
  297.9 12.9 %collective-permute-start.99 = (f32[1,8,16]{2,1,0:T(8,128)S(1)}, f32[1,8,16]{2,1,0:T(8,128)S(1)}, u32[]{:S(2)}, u32[]{:S(2)}) collective-permute-start(f32[1,8,16]{2,1,0:T(8,128)S(1)} %add.950), channel_id=1, source_target_pairs={{0,4},{2,6},{4,8},{6,10},{8,12},{10,14},{12,16},{14,18},{16,20},{1... | collective-permute-start | bytes 1544 | tf_op jit(solution)/shard_map/ppermute | solution.py:30
  303.3 7.5 %collective-permute-start.100 = (f32[1,8,16]{2,1,0:T(8,128)S(1)}, f32[1,8,16]{2,1,0:T(8,128)S(1)}, u32[]{:S(2)}, u32[]{:S(2)}) collective-permute-start(f32[1,8,16]{2,1,0:T(8,128)S(1)} %add.950), channel_id=1, source_target_pairs={{4,0},{6,2},{8,4},{10,6},{12,8},{14,10},{16,12},{18,14},{20,16},{2... | collective-permute-start | bytes 1544 | tf_op jit(solution)/shard_map/ppermute | solution.py:30
  310.9 11.9 %collective-permute-start.104 = (f32[1,8,16]{2,1,0:T(8,128)S(1)}, f32[1,8,16]{2,1,0:T(8,128)S(1)}, u32[]{:S(2)}, u32[]{:S(2)}) collective-permute-start(f32[1,8,16]{2,1,0:T(8,128)S(1)} %fusion.169), channel_id=1, source_target_pairs={{4,0},{6,2},{8,4},{10,6},{12,8},{14,10},{16,12},{18,14},{20,16},{2... | collective-permute-start | bytes 1544 | tf_op jit(solution)/shard_map/ppermute | solution.py:30
  312.8 10.0 %collective-permute-start.103 = (f32[1,8,16]{2,1,0:T(8,128)S(1)}, f32[1,8,16]{2,1,0:T(8,128)S(1)}, u32[]{:S(2)}, u32[]{:S(2)}) collective-permute-start(f32[1,8,16]{2,1,0:T(8,128)S(1)} %fusion.169), channel_id=1, source_target_pairs={{0,4},{2,6},{4,8},{6,10},{8,12},{10,14},{12,16},{14,18},{16,20},{1... | collective-permute-start | bytes 1544 | tf_op jit(solution)/shard_map/ppermute | solution.py:30
  323.1 12.5 %collective-permute-start.107 = (f32[1,16,32]{2,1,0:T(8,128)S(1)}, f32[1,16,32]{2,1,0:T(8,128)S(1)}, u32[]{:S(2)}, u32[]{:S(2)}) collective-permute-start(f32[1,16,32]{2,1,0:T(8,128)S(1)} %add.964), channel_id=1, source_target_pairs={{0,2},{2,4},{4,6},{6,8},{8,10},{10,12},{12,14},{14,16},{16,18},{18... | collective-permute-start | bytes 6152 | tf_op jit(solution)/shard_map/ppermute | solution.py:30
  328.2 7.4 %collective-permute-start.108 = (f32[1,16,32]{2,1,0:T(8,128)S(1)}, f32[1,16,32]{2,1,0:T(8,128)S(1)}, u32[]{:S(2)}, u32[]{:S(2)}) collective-permute-start(f32[1,16,32]{2,1,0:T(8,128)S(1)} %add.964), channel_id=1, source_target_pairs={{2,0},{4,2},{6,4},{8,6},{10,8},{12,10},{14,12},{16,14},{18,16},{20... | collective-permute-start | bytes 6152 | tf_op jit(solution)/shard_map/ppermute | solution.py:30
  335.6 13.1 %collective-permute-start.112 = (f32[1,16,32]{2,1,0:T(8,128)S(1)}, f32[1,16,32]{2,1,0:T(8,128)S(1)}, u32[]{:S(2)}, u32[]{:S(2)}) collective-permute-start(f32[1,16,32]{2,1,0:T(8,128)S(1)} %fusion.128), channel_id=1, source_target_pairs={{2,0},{4,2},{6,4},{8,6},{10,8},{12,10},{14,12},{16,14},{18,16},{20... | collective-permute-start | bytes 6152 | tf_op jit(solution)/shard_map/ppermute | solution.py:30
  338.7 10.0 %collective-permute-start.111 = (f32[1,16,32]{2,1,0:T(8,128)S(1)}, f32[1,16,32]{2,1,0:T(8,128)S(1)}, u32[]{:S(2)}, u32[]{:S(2)}) collective-permute-start(f32[1,16,32]{2,1,0:T(8,128)S(1)} %fusion.128), channel_id=1, source_target_pairs={{0,2},{2,4},{4,6},{6,8},{8,10},{10,12},{12,14},{14,16},{16,18},{18... | collective-permute-start | bytes 6152 | tf_op jit(solution)/shard_map/ppermute | solution.py:30
  349.0 12.8 %collective-permute-start.118 = (f32[1,32,64]{2,1,0:T(8,128)S(1)}, f32[1,32,64]{2,1,0:T(8,128)S(1)}, u32[]{:S(2)}, u32[]{:S(2)}) collective-permute-start(f32[1,32,64]{2,1,0:T(8,128)S(1)} %get-tuple-element.42), channel_id=1, source_target_pairs={{2,0},{4,2},{6,4},{8,6},{10,8},{12,10},{14,12},{16,14},{18,16},{20... | collective-permute-start | bytes 24584 | tf_op jit(solution)/shard_map/ppermute | solution.py:30
  350.9 10.9 %collective-permute-start.115 = (f32[1,32,64]{2,1,0:T(8,128)S(1)}, f32[1,32,64]{2,1,0:T(8,128)S(1)}, u32[]{:S(2)}, u32[]{:S(2)}) collective-permute-start(f32[1,32,64]{2,1,0:T(8,128)S(1)} %get-tuple-element.41), channel_id=1, source_target_pairs={{0,2},{2,4},{4,6},{6,8},{8,10},{10,12},{12,14},{14,16},{16,18},{18... | collective-permute-start | bytes 24584 | tf_op jit(solution)/shard_map/ppermute | solution.py:30
  361.9 12.8 %collective-permute-start.122 = (f32[1,32,64]{2,1,0:T(8,128)S(1)}, f32[1,32,64]{2,1,0:T(8,128)S(1)}, u32[]{:S(2)}, u32[]{:S(2)}) collective-permute-start(f32[1,32,64]{2,1,0:T(8,128)S(1)} %get-tuple-element.38), channel_id=1, source_target_pairs={{2,0},{4,2},{6,4},{8,6},{10,8},{12,10},{14,12},{16,14},{18,16},{20... | collective-permute-start | bytes 24584 | tf_op jit(solution)/shard_map/ppermute | solution.py:30
  363.8 10.9 %collective-permute-start.119 = (f32[1,32,64]{2,1,0:T(8,128)S(1)}, f32[1,32,64]{2,1,0:T(8,128)S(1)}, u32[]{:S(2)}, u32[]{:S(2)}) collective-permute-start(f32[1,32,64]{2,1,0:T(8,128)S(1)} %get-tuple-element.37), channel_id=1, source_target_pairs={{0,2},{2,4},{4,6},{6,8},{8,10},{10,12},{12,14},{14,16},{16,18},{18... | collective-permute-start | bytes 24584 | tf_op jit(solution)/shard_map/ppermute | solution.py:30
  375.2 12.8 %collective-permute-start.126 = (f32[1,64,128]{2,1,0:T(8,128)S(1)}, f32[1,64,128]{2,1,0:T(8,128)S(1)}, u32[]{:S(2)}, u32[]{:S(2)}) collective-permute-start(f32[1,64,128]{2,1,0:T(8,128)S(1)} %get-tuple-element.22), channel_id=1, source_target_pairs={{2,0},{4,2},{6,4},{8,6},{10,8},{12,10},{14,12},{16,14},{18,16},{20... | collective-permute-start | bytes 98312 | tf_op jit(solution)/shard_map/ppermute | solution.py:30
  377.2 10.9 %collective-permute-start.123 = (f32[1,64,128]{2,1,0:T(8,128)S(1)}, f32[1,64,128]{2,1,0:T(8,128)S(1)}, u32[]{:S(2)}, u32[]{:S(2)}) collective-permute-start(f32[1,64,128]{2,1,0:T(8,128)S(1)} %get-tuple-element.21), channel_id=1, source_target_pairs={{0,2},{2,4},{4,6},{6,8},{8,10},{10,12},{12,14},{14,16},{16,18},{18... | collective-permute-start | bytes 98312 | tf_op jit(solution)/shard_map/ppermute | solution.py:30
  388.3 12.8 %collective-permute-start.130 = (f32[1,64,128]{2,1,0:T(8,128)S(1)}, f32[1,64,128]{2,1,0:T(8,128)S(1)}, u32[]{:S(2)}, u32[]{:S(2)}) collective-permute-start(f32[1,64,128]{2,1,0:T(8,128)S(1)} %get-tuple-element.18), channel_id=1, source_target_pairs={{2,0},{4,2},{6,4},{8,6},{10,8},{12,10},{14,12},{16,14},{18,16},{20... | collective-permute-start | bytes 98312 | tf_op jit(solution)/shard_map/ppermute | solution.py:30
  390.2 10.9 %collective-permute-start.127 = (f32[1,64,128]{2,1,0:T(8,128)S(1)}, f32[1,64,128]{2,1,0:T(8,128)S(1)}, u32[]{:S(2)}, u32[]{:S(2)}) collective-permute-start(f32[1,64,128]{2,1,0:T(8,128)S(1)} %get-tuple-element.17), channel_id=1, source_target_pairs={{0,2},{2,4},{4,6},{6,8},{8,10},{10,12},{12,14},{14,16},{16,18},{18... | collective-permute-start | bytes 98312 | tf_op jit(solution)/shard_map/ppermute | solution.py:30
  401.3 12.8 %collective-permute-start.134 = (f32[1,64,128]{2,1,0:T(8,128)S(1)}, f32[1,64,128]{2,1,0:T(8,128)S(1)}, u32[]{:S(2)}, u32[]{:S(2)}) collective-permute-start(f32[1,64,128]{2,1,0:T(8,128)S(1)} %get-tuple-element.14), channel_id=1, source_target_pairs={{2,0},{4,2},{6,4},{8,6},{10,8},{12,10},{14,12},{16,14},{18,16},{20... | collective-permute-start | bytes 98312 | tf_op jit(solution)/shard_map/ppermute | solution.py:30
  403.3 10.9 %collective-permute-start.131 = (f32[1,64,128]{2,1,0:T(8,128)S(1)}, f32[1,64,128]{2,1,0:T(8,128)S(1)}, u32[]{:S(2)}, u32[]{:S(2)}) collective-permute-start(f32[1,64,128]{2,1,0:T(8,128)S(1)} %get-tuple-element.13), channel_id=1, source_target_pairs={{0,2},{2,4},{4,6},{6,8},{8,10},{10,12},{12,14},{14,16},{16,18},{18... | collective-permute-start | bytes 98312 | tf_op jit(solution)/shard_map/ppermute | solution.py:30
  (72 other events, 238.6 us)
where the time goes:
time: 418 us; the launch traced here: 415 us
  starting transfers between devices  330 us (79%)
  waiting for transfers between devices  66 us (16%)
  other arithmetic  8.52 us (2%)
  local copies, waits for them, and re-layouts  7.62 us (2%)
    ppermute x55, starting transfers between devices, from_behind(): return lax.ppermute(block, axis, route)  168 us
    ppermute x32, starting transfers between devices, padded(): lax.ppermute(lax.slice_in_dim(block, 0, width, axis=dim), axis, backward)  104 us
    ppermute x32, starting transfers between devices, padded(): lax.ppermute(lax.slice_in_dim(block, block.shape[dim] - width, None, axis...  44.9 us
    ppermute x32, waiting for transfers between devices, padded(): lax.ppermute(lax.slice_in_dim(block, block.shape[dim] - width, None, axis...  30.6 us
    ppermute x16, waiting for transfers between devices, partner_2(): return lax.ppermute(value, axis, pairs)  27.6 us
    ppermute x16, starting transfers between devices, partner_2(): return lax.ppermute(value, axis, pairs)  13.3 us
  transfers between devices with their start and end apart: 135, of which 45 were waited for; matrix products, arithmetic and copies ran while one was open for 1% of the time, Pallas kernels for 0%

commit v1 on v0

v1 whole, which is shorter than its diff:
```python
import functools

import jax
import jax.numpy as jnp
import numpy as np
from jax import lax
from jax.experimental import pallas as pl
from jax.experimental.pallas import tpu as pltpu
from jax.sharding import PartitionSpec as P

LEVELS = 6
NU = 2
COARSE_SWEEPS = 6
OMEGA = 0.8
LIQUID, GAS = 1.0, 1000.0
MIXED = float(np.asarray(2.0 * LIQUID * GAS / (LIQUID + GAS), jnp.bfloat16))
MESH = pl.DeviceIdType.MESH
REACH = 3
EDGE = 8
EDGE_PHASE = 16
UNROLL = 16
LARGE = 1 << 20


def each(count, body):
    if count <= UNROLL:
        for i in range(count):
            body(i)
    else:
        lax.fori_loop(0, count, lambda i, carry: (body(i), carry)[1], 0)


def index_along(shape, axis):
    return lax.broadcasted_iota(jnp.int32, shape, axis)


def roll(x, shift, axis):
    return pltpu.roll(x, shift % x.shape[axis], axis)


def lane_bit(x, step):
    return index_along(x.shape, x.ndim - 1) // step % 2


def even_part(x, step):
    return jnp.where(lane_bit(x, step) == 0, x, roll(x, step, x.ndim - 1))


def odd_part(x, step):
    return jnp.where(lane_bit(x, step) == 1, x, roll(x, -step, x.ndim - 1))


def pair_lanes(x, step):
    axis = x.ndim - 1
    return x + jnp.where(lane_bit(x, step) == 0, roll(x, -step, axis), roll(x, step, axis))


def harmonic(a, b):
    low, high = jnp.minimum(a, b), jnp.maximum(a, b)
    return jnp.where((low == 0.0) | (low == high), high, MIXED)


def store(ref, i, value):
    ref[i] = value.astype(ref.dtype)


def wide(ref, i):
    return ref[i].astype(jnp.float32)


def quarter(x):
    return (0.25 * x).astype(jnp.bfloat16).astype(jnp.float32)


def kernel(ngx, ngy, counts, f_ref, phase_ref, scaled_ref, rest_ref, *refs):
    gx, gy = lax.axis_index("gx"), lax.axis_index("gy")
    n = ngx * ngy
    me = gx * ngy + gy
    lx, ly, nz = f_ref.shape
    by, cy = ly // 2, ly // 4
    refs = list(refs)

    def take(count):
        out = refs[:count]
        del refs[:count]
        return out

    (w0, wp, w1, gp, g2, p_pack, g1_pack, g2_pack, temp) = take(9)
    (b1, e2) = take(2)
    level_refs = [take(10) for _ in range(LEVELS + 1)]
    (s0, r0, s1, r1, sp, rp, sg, rg) = take(8)

    w0[...] = jnp.zeros(w0.shape, w0.dtype)
    wp[...] = jnp.zeros(wp.shape, wp.dtype)
    w1[...] = jnp.zeros(w1.shape, w1.dtype)

    barrier = pltpu.get_barrier_semaphore()

    def greet(k, carry):
        other = (me + k) % n
        pl.semaphore_signal(barrier, inc=1, device_id=(other // ngy, other % ngy), device_id_type=MESH)
        return carry

    lax.fori_loop(1, n, greet, 0)

    for plane in range(0, lx, 4):
        beta = [
            jnp.where(phase_ref[plane + 2 * k, pl.ds(0, by, 2), :] == 1, GAS, LIQUID) for k in range(2)
        ]
        p_pack[0] = jnp.where(lane_bit(beta[0], 1) == 0, beta[0], beta[1]).astype(jnp.bfloat16)
    for l in range(LEVELS + 1):
        for v in level_refs[l][:2]:
            zero = jnp.zeros(v.shape[1:], v.dtype)
            v[0] = zero
            v[v.shape[0] - 1] = zero

    pl.semaphore_wait(barrier, n - 1)

    def window_copy(src, dst, send, recv, reach, edge, d, e, slot, low_row):
        lead, rows = src.shape[0], src.shape[1]
        count = rows if e == 0 else edge
        source = src.at[:, pl.ds(rows - edge if e == 1 else 0, count), :]
        start = {0: edge, 1: 0, -1: edge + rows}[low_row]
        target = dst.at[pl.ds(slot * lead, lead), pl.ds(start, count), :]
        k = (d + reach) * 3 + e + 1
        return pltpu.make_async_remote_copy(
            src_ref=source, dst_ref=target, send_sem=send.at[k], recv_sem=recv.at[slot * 3 + 1 - low_row],
            device_id=(gx + d, gy + e), device_id_type=MESH,
        )

    def window(reach):
        for e in (0, 1, -1):
            for d in sorted(range(-reach, reach + 1), key=abs):
                if (d, e) != (0, 0):
                    there = (gx + d >= 0) & (gx + d < ngx) & (gy + e >= 0) & (gy + e < ngy)
                    yield d, e, there

    def window_send(src, dst, send, recv, reach, edge):
        for d, e, there in window(reach):
            @pl.when(there)
            def _():
                window_copy(src, dst, send, recv, reach, edge, d, e, reach - d, e).start()

    def window_wait(src, dst, send, recv, reach, edge):
        for d, e, there in window(reach):
            @pl.when(there)
            def _():
                window_copy(src, dst, send, recv, reach, edge, d, e, reach + d, -e).wait_recv()

    def window_done(src, dst, send, recv, reach, edge):
        for d, e, there in window(reach):
            @pl.when(there)
            def _():
                window_copy(src, dst, send, recv, reach, edge, d, e, reach - d, e).wait_send()

    def gather_send(src, dst, k):
        def body(t, carry):
            other = (me + t) % n
            pltpu.make_async_remote_copy(
                src_ref=src, dst_ref=dst.at[pl.ds(me, 1)], send_sem=sg.at[k], recv_sem=rg.at[k],
                device_id=(other // ngy, other % ngy), device_id_type=MESH,
            ).start()
            return carry

        lax.fori_loop(1, n, body, 0)

    def gather_all(dst, k):
        every = dst.at[pl.ds(0, n - 1)]
        return pltpu.make_async_remote_copy(
            src_ref=every, dst_ref=every, send_sem=sg.at[k], recv_sem=rg.at[k],
            device_id=(gx, (gy + 1) % ngy), device_id_type=MESH,
        )

    phase_window = (p_pack, wp, sp, rp, REACH, EDGE_PHASE)
    fine_window = (f_ref, w0, s0, r0, 1, EDGE)
    coarse_window = (g1_pack, w1, s1, r1, REACH, EDGE)
    window_send(*phase_window)
    window_send(*fine_window)
    gather_send(p_pack, gp, 0)

    wp[REACH, pl.ds(EDGE_PHASE, by), :] = p_pack[0]
    gp[me] = p_pack[0]
    w0[pl.ds(lx, lx), pl.ds(EDGE, ly), :] = f_ref[...]

    slots = temp.shape[0]

    def stretch(value, slot):
        rows = value.shape[0]
        temp[slot, pl.ds(0, rows, 2), :] = value
        temp[slot, pl.ds(1, rows, 2), :] = value

    def pair_rows(value, slot, first=True, second=True):
        rows = value.shape[0]
        temp[slot, pl.ds(0, rows), :] = value
        out = 0.0
        if first:
            out = out + temp[slot, pl.ds(0, rows // 2, 2), :]
        if second:
            out = out + temp[slot, pl.ds(1, rows // 2, 2), :]
        return out

    def neighbours(level, v_ref, i, step):
        (_, _, _, _, _, fx, fyl, fyh, fzl, fzh) = level
        v = v_ref[i + 1]
        return (
            wide(fx, i) * v_ref[i] + wide(fx, i + 1) * v_ref[i + 2]
            + wide(fyl, i) * roll(v, 1, 0) + wide(fyh, i) * roll(v, -1, 0)
            + wide(fzl, i) * roll(v, step, 1) + wide(fzh, i) * roll(v, -step, 1)
        )

    def sweep(level, source, target, step, first, last):
        f, inverse = level[2], level[3]

        def body(k):
            i = k + first
            target[i + 1] = (1.0 - OMEGA) * source[i + 1] + inverse[i] * (f[i] + neighbours(level, source, i, step))

        each(last - first, body)

    def rest_of(level, v_ref, i, step):
        return level[2][i] - level[4][i] * v_ref[i + 1] + neighbours(level, v_ref, i, step)

    def put_faces(level, i, inside, lows, step, edges):
        (_, _, _, inverse, centre, fx, fyl, fyh, fzl, fzh) = level
        (yl, yh, zl, zh) = lows
        total = wide(fx, i) + wide(fx, i + 1) + yl + yh + zl + zh
        inverse[i] = jnp.where(inside, OMEGA / jnp.where(inside, total, 1.0), 0.0)
        centre[i] = total
        lane = index_along(zl.shape, 1)
        fzl[i] = jnp.where(lane < step, 0.0, zl).astype(fzl.dtype)
        fzh[i] = jnp.where(lane >= nz - step, 0.0, zh).astype(fzh.dtype)
        if edges is not None:
            row = index_along(yl.shape, 0)
            yl = jnp.where(row == 0, 0.0, yl)
            yh = jnp.where(row >= edges - 1, 0.0, yh)
        fyl[i] = yl.astype(fyl.dtype)
        fyh[i] = yh.astype(fyh.dtype)

    def cell_faces(b, step):
        lane = index_along(b.shape, 1)
        yl, yh = harmonic(roll(b, 1, 0), b), harmonic(b, roll(b, -1, 0))
        zl = harmonic(jnp.where(lane < step, 0.0, roll(b, step, 1)), b)
        zh = harmonic(b, jnp.where(lane >= nz - step, 0.0, roll(b, -step, 1)))
        return yl, yh, zl, zh

    window_wait(*phase_window)
    for t in range(2 * REACH + 1):
        packed = wp[t].astype(jnp.float32)[EDGE_PHASE - EDGE : EDGE_PHASE + by + EDGE]
        b1[2 * t] = even_part(packed, 1)
        b1[2 * t + 1] = odd_part(packed, 1)

    level0 = level_refs[0]
    (va, vb, f0, inv0, c0, fx0) = level0[:6]
    rows0 = ly + 2 * EDGE
    blocks = 3 * lx // 2
    first_block = 2 * REACH - lx // 2
    before = None
    beta0 = []
    for j in range(-1, blocks + 1):
        stretch(b1[first_block + j], (j + 1) % slots)
        b = temp[(j + 1) % slots, pl.ds(EDGE, rows0), :]
        if before is not None:
            fx0[2 * j] = harmonic(before, b)
        if 0 <= j < blocks:
            fx0[2 * j + 1] = b
            beta0.append(b)
        before = b
    for j in range(blocks):
        lows = cell_faces(beta0[j], 1)
        for i in (2 * j, 2 * j + 1):
            put_faces(level0, i, beta0[j] > 0.0, lows, 1, None)

    window_wait(*fine_window)
    level0 = list(level0)
    level0[2] = w0
    planes0 = 3 * lx
    for i in range(planes0):
        va[i + 1] = inv0[i] * w0[i]
    sweep(level0, va, vb, 1, 1, planes0 - 1)
    rests = [rest_of(level0, vb, lx + i, 1)[EDGE : EDGE + ly] for i in range(lx)]
    coarse = [
        0.5 * pair_lanes(pair_rows(rests[2 * k] + rests[2 * k + 1], k % slots), 1) for k in range(lx // 2)
    ]
    packed = jnp.where(lane_bit(coarse[0], 1) == 0, coarse[0], coarse[1])
    g1_pack[0] = packed
    window_send(*coarse_window)
    w1[REACH, pl.ds(EDGE, by), :] = packed

    level1 = level_refs[1]
    (ua, ub, f1, inv1, c1, fx1) = level1[:6]
    planes1 = 2 * (2 * REACH + 1)
    fx1[0] = b1[0]
    fx1[planes1] = b1[planes1 - 1]
    for i in range(1, planes1):
        fx1[i] = harmonic(b1[i - 1], b1[i])
    for i in range(planes1):
        put_faces(level1, i, b1[i] > 0.0, cell_faces(b1[i], 2), 2, None)

    gather_all(gp, 0).wait_recv()

    def whole_plane(ref, k):
        parts = [ref[k * ngy + j].astype(jnp.float32) for j in range(ngy)]
        return jnp.concatenate(parts, axis=0)

    shape2 = counts[2]
    (nx2, ny2) = shape2
    level2 = level_refs[2]
    row1 = index_along((2 * ny2, nz), 0)

    raw = {}
    for l in range(2, LEVELS + 1):
        raw[l] = level_refs[l][6:10]

    def faces2(i):
        pack = whole_plane(gp, i)
        b = [even_part(pack, 1), odd_part(pack, 1)]
        if isinstance(i, int):
            below = odd_part(whole_plane(gp, i - 1), 1) if i > 0 else jnp.zeros_like(b[0])
        else:
            below = jnp.where(i > 0, odd_part(whole_plane(gp, jnp.maximum(i - 1, 0)), 1), 0.0)
        slot = 4 * (i % 2)
        store(level2[5], i, quarter(pair_lanes(pair_rows(harmonic(below, b[0]), slot), 2)))
        last = row1 == 2 * ny2 - 1
        yl = sum(harmonic(jnp.where(row1 == 0, 0.0, roll(x, 1, 0)), x) for x in b)
        yh = sum(harmonic(x, jnp.where(last, 0.0, roll(x, -1, 0))) for x in b)
        lane = index_along(b[0].shape, 1)
        zl = sum(harmonic(jnp.where(lane < 2, 0.0, roll(x, 2, 1)), x) for x in b)
        zh = sum(harmonic(x, jnp.where(lane >= nz - 2, 0.0, roll(x, -2, 1))) for x in b)
        store(raw[2][0], i, quarter(pair_lanes(pair_rows(yl, slot + 1, second=False), 2)))
        store(raw[2][1], i, quarter(pair_lanes(pair_rows(yh, slot + 2, first=False), 2)))
        store(raw[2][2], i, quarter(even_part(pair_rows(zl, slot + 3), 2)))
        store(raw[2][3], i, quarter(odd_part(pair_rows(zh, slot), 2)))

    each(nx2, faces2)
    top = odd_part(whole_plane(gp, nx2 - 1), 1)
    store(level2[5], nx2, quarter(pair_lanes(pair_rows(top, 5), 2)))

    for l in range(2, LEVELS + 1):
        nx, ny = counts[l]
        step = 2**l
        level = level_refs[l]
        if l < LEVELS:
            finer, coarser = level_refs[l], level_refs[l + 1]
            size = max(ny // 2, 4)
            if ny // 2 < EDGE:
                for ref in coarser[5:10]:
                    ref[...] = jnp.zeros(ref.shape, ref.dtype)

            def put(ref, i, value):
                ref[i, pl.ds(0, size), :] = quarter(value).astype(ref.dtype)

            def coarsen(i):
                slot = 4 * (i % 2)
                (fx, yl, yh, zl, zh) = finer[5:10]
                a, b = 2 * i, 2 * i + 1
                put(coarser[5], i, pair_lanes(pair_rows(wide(fx, a), slot), step))
                put(coarser[6], i, pair_lanes(pair_rows(wide(yl, a) + wide(yl, b), slot + 1, second=False), step))
                put(coarser[7], i, pair_lanes(pair_rows(wide(yh, a) + wide(yh, b), slot + 2, first=False), step))
                put(coarser[8], i, even_part(pair_rows(wide(zl, a) + wide(zl, b), slot + 3), step))
                put(coarser[9], i, odd_part(pair_rows(wide(zh, a) + wide(zh, b), slot), step))

            each(nx // 2, coarsen)
            put(coarser[5], nx // 2, pair_lanes(pair_rows(wide(finer[5], nx), 5), step))

        def finish(i):
            lows = [wide(ref, i) for ref in level[6:10]]
            inside = index_along(lows[0].shape, 0) < ny
            put_faces(level, i, inside, lows, step, ny)

        each(nx, finish)

    window_wait(*coarse_window)
    for t in range(2 * REACH + 1):
        f1[2 * t] = even_part(w1[t], 1)
        f1[2 * t + 1] = odd_part(w1[t], 1)
    for i in range(planes1):
        ua[i + 1] = inv1[i] * f1[i]
    sweep(level1, ua, ub, 2, 1, planes1 - 1)
    rests = [rest_of(level1, ub, 2 * REACH + i, 2)[EDGE : EDGE + by] for i in range(2)]
    coarse = 0.5 * pair_lanes(pair_rows(rests[0] + rests[1], 0), 2)
    half = cy // 2
    packed = jnp.where(lane_bit(coarse[:half], 1) == 0, coarse[:half], coarse[half:])
    g2_pack[0] = packed
    gather_send(g2_pack, g2, 1)
    g2[me] = packed
    gather_all(g2, 1).wait_recv()

    f2 = level2[2]

    def unpack(i):
        parts = []
        for j in range(ngy):
            pack = g2[i * ngy + j]
            parts += [even_part(pack, 1), odd_part(pack, 1)]
        f2[i] = jnp.concatenate(parts, axis=0)

    each(nx2, unpack)

    def cycle(l):
        nx, ny = counts[l]
        step = 2**l
        level = level_refs[l]
        (xa, xb, f, inverse) = level[:4]

        def begin(i):
            xa[i + 1] = inverse[i] * f[i]

        each(nx, begin)
        if l == LEVELS:
            for repeat in range(COARSE_SWEEPS - 1):
                sweep(level, xa, xb, step, 0, nx)
                xa, xb = xb, xa
            return xa
        for repeat in range(NU - 1):
            sweep(level, xa, xb, step, 0, nx)
            xa, xb = xb, xa
        f_next = level_refs[l + 1][2]
        size = max(ny // 2, 4)
        if ny // 2 < EDGE:
            f_next[...] = jnp.zeros(f_next.shape, f_next.dtype)

        def restrict(i):
            r = rest_of(level, xa, 2 * i, step) + rest_of(level, xa, 2 * i + 1, step)
            f_next[i, pl.ds(0, size), :] = 0.5 * pair_lanes(pair_rows(r, i % slots), step)

        each(nx // 2, restrict)
        fine = cycle(l + 1)

        def correct(i):
            slot = i % slots
            stretch(fine[i + 1], slot)
            e = temp[slot, pl.ds(0, xa.shape[1]), :]
            xb[2 * i + 1] = xa[2 * i + 1] + e
            xb[2 * i + 2] = xa[2 * i + 2] + e

        each(nx // 2, correct)
        xa, xb = xb, xa
        for repeat in range(NU):
            sweep(level, xa, xb, step, 0, nx)
            xa, xb = xb, xa
        return xa

    found = cycle(2)

    row2 = pl.multiple_of(gy * cy, 8)
    below2 = pl.multiple_of(jnp.maximum(gy * cy - EDGE, 0), 8)
    above2 = pl.multiple_of(jnp.minimum(gy * cy + cy, ny2 - EDGE), 8)
    for t in range(2 * REACH + 1):
        x = gx + t - REACH
        there = (x >= 0) & (x < nx2)
        plane = jnp.clip(x, 0, nx2 - 1) + 1
        e2[t, pl.ds(EDGE, cy), :] = jnp.where(there, found[plane, pl.ds(row2, cy), :], 0.0)
        low = found[plane, pl.ds(below2, EDGE), :]
        high = found[plane, pl.ds(above2, EDGE), :]
        e2[t, pl.ds(0, EDGE), :] = jnp.where(there & (gy > 0), low, 0.0)
        e2[t, pl.ds(EDGE + cy, EDGE), :] = jnp.where(there & (gy < ngy - 1), high, 0.0)

    for t in range(2 * REACH + 1):
        slot = t % slots
        stretch(e2[t], slot)
        e = temp[slot, pl.ds(EDGE, by + 2 * EDGE), :]
        ua[2 * t + 1] = ub[2 * t + 1] + e
        ua[2 * t + 2] = ub[2 * t + 2] + e
    sweep(level1, ua, ub, 2, 2, planes1 - 2)
    sweep(level1, ub, ua, 2, 3, planes1 - 3)

    for j in range(blocks):
        slot = j % slots
        stretch(ua[first_block + j + 1], slot)
        e = temp[slot, pl.ds(EDGE, rows0), :]
        va[2 * j + 1] = vb[2 * j + 1] + e
        va[2 * j + 2] = vb[2 * j + 2] + e
    sweep(level0, va, vb, 1, 2, planes0 - 2)
    sweep(level0, vb, va, 1, 3, planes0 - 3)
    for i in range(lx):
        product = c0[lx + i] * va[lx + i + 1]
        near = neighbours(level0, va, lx + i, 1)
        own = slice(EDGE, EDGE + ly)
        scaled_ref[i] = product[own]
        rest_ref[i] = w0[lx + i, pl.ds(EDGE, ly), :] - product[own] + near[own]

    window_done(*phase_window)
    window_done(*fine_window)
    window_done(*coarse_window)
    gather_all(gp, 0).wait_send()
    gather_all(g2, 1).wait_send()


def solution(mesh):
    ngx, ngy = mesh.shape["gx"], mesh.shape["gy"]
    n = ngx * ngy

    def on_device(right_side, phase):
        lx, ly, nz = right_side.shape
        assert lx == 4 and ly % 32 == 0 and NU == 2
        by, cy = ly // 2, ly // 4
        counts = [(lx * ngx >> l, ly * ngy >> l) for l in range(LEVELS + 1)]
        blocks = 2 * REACH + 1

        def level_scratch(planes, rows, padded_source=False):
            shapes = [planes + 2, planes + 2, planes, planes, planes, planes + 1] + [planes] * 4
            if padded_source:
                shapes[2] = 1
            large = planes * rows * nz * 4 >= LARGE
            types = [jnp.float32] * 5 + [jnp.bfloat16 if large else jnp.float32] * 5
            return [pltpu.VMEM((k, rows, nz), dtype) for k, dtype in zip(shapes, types)]

        scratch = [
            pltpu.VMEM((3 * lx, ly + 2 * EDGE, nz), jnp.float32),
            pltpu.VMEM((blocks, by + 2 * EDGE_PHASE, nz), jnp.bfloat16),
            pltpu.VMEM((blocks, by + 2 * EDGE, nz), jnp.float32),
            pltpu.VMEM((n, by, nz), jnp.bfloat16),
            pltpu.VMEM((n, cy // 2, nz), jnp.float32),
            pltpu.VMEM((1, by, nz), jnp.bfloat16),
            pltpu.VMEM((1, by, nz), jnp.float32),
            pltpu.VMEM((1, cy // 2, nz), jnp.float32),
            pltpu.VMEM((8, max(2 * (by + 2 * EDGE), 2 * counts[2][1], 2 * (cy + 2 * EDGE)), nz), jnp.float32),
            pltpu.VMEM((2 * blocks, by + 2 * EDGE, nz), jnp.float32),
            pltpu.VMEM((blocks, cy + 2 * EDGE, nz), jnp.float32),
        ]
        scratch += level_scratch(3 * lx, ly + 2 * EDGE, True)
        scratch += level_scratch(2 * blocks, by + 2 * EDGE)
        for l in range(2, LEVELS + 1):
            scratch += level_scratch(counts[l][0], max(counts[l][1], EDGE))
        scratch += [pltpu.SemaphoreType.DMA((9,))] * 2
        scratch += [pltpu.SemaphoreType.DMA((3 * blocks,))] * 4
        scratch += [pltpu.SemaphoreType.DMA((2,))] * 2
        return pl.pallas_call(
            functools.partial(kernel, ngx, ngy, counts),
            out_shape=[jax.ShapeDtypeStruct(right_side.shape, jnp.float32)] * 2,
            in_specs=[pl.BlockSpec(memory_space=pltpu.VMEM)] * 2,
            out_specs=[pl.BlockSpec(memory_space=pltpu.VMEM)] * 2,
            scratch_shapes=scratch,
            compiler_params=pltpu.CompilerParams(
                collective_id=0, has_side_effects=True, vmem_limit_bytes=66_000_000
            ),
        )(right_side, phase)

    placed = P("gx", "gy", None)
    return jax.shard_map(
        on_device, mesh=mesh, in_specs=(placed, placed), out_specs=(placed, placed), check_vma=False
    )
```

time: 418 us -> 37.5 us (0.09)
  the two profiles are of different devices: /device:TPU:7 before, /device:TPU:0 now
where the time goes in v1:
time: 37.5 us; the launch traced here: 37.3 us
  Pallas kernels  34.4 us (92%)
  local copies, waits for them, and re-layouts  2.26 us (6%)
  between operations  0.65 us (2%)
    pallas_call x1, Pallas kernels, on_device(): pl.pallas_call(functools.partial(kernel, ngx, ngy, counts), out_shape=[ja...  34.4 us
    unnamed x4, local copies, waits for them, and re-layouts  2.26 us

profile of v1, /device:TPU:0, one launch (start us, length us, event | category | flops | bytes accessed | tf_op | source)
XLA Modules:
  0.0 37.3 jit_solution(7686577264434893462)
XLA Ops:
  0.6 34.4 %shard_map.41 = (f32[4,64,128]{2,1,0:T(8,128)}, f32[4,64,128]{2,1,0:T(8,128)}) custom-call(f32[4,64,128]{2,1,0:T(8,128)} %f_ref.1, s32[4,64,128]{2,1,0:T(8,128)} %phase_ref.1), custom_call_target="tpu_custom_call" | custom-call | tf_op jit(solution)/shard_map/pallas_call | solution.py:528
  35.1 0.0 copy-start
  35.1 1.6 %copy.6 = f32[4,64,128]{2,1,0:T(8,128)} copy(f32[4,64,128]{2,1,0:T(8,128)} %get-tuple-element.4) | data formatting | bytes 262144
  36.7 0.0 copy-done
  36.7 0.7 %copy.7 = f32[4,64,128]{2,1,0:T(8,128)} copy(f32[4,64,128]{2,1,0:T(8,128)S(1)} %copy-done) | data formatting | bytes 262144
Async XLA Ops:
  35.1 1.6 %copy-start = (f32[4,64,128]{2,1,0:T(8,128)S(1)}, f32[4,64,128]{2,1,0:T(8,128)}, u32[]{:S(2)}) copy-start(f32[4,64,128]{2,1,0:T(8,128)} %get-tuple-element.5) | copy-start | bytes 393220

commit v2 on v1

--- a/solution.py
+++ b/solution.py
@@ -88,7 +88,7 @@
     (w0, wp, w1, gp, g2, p_pack, g1_pack, g2_pack, temp) = take(9)
     (b1, e2) = take(2)
     level_refs = [take(10) for _ in range(LEVELS + 1)]
-    (s0, r0, s1, r1, sp, rp, sg, rg) = take(8)
+    (s0, r0, sf, rf, s1, r1, sp, rp, sg, rg) = take(10)
 
     w0[...] = jnp.zeros(w0.shape, w0.dtype)
     wp[...] = jnp.zeros(wp.shape, wp.dtype)
@@ -116,42 +116,49 @@
 
     pl.semaphore_wait(barrier, n - 1)
 
-    def window_copy(src, dst, send, recv, reach, edge, d, e, slot, low_row):
+    def window_copy(src, dst, send, recv, reach, edge, half, d, e, slot, low_row, toward):
         lead, rows = src.shape[0], src.shape[1]
+        plane, planes = 0, lead
+        if half is not None and d != 0:
+            planes = lead // 2
+            plane = planes if (toward > 0) == (half == 0) else 0
         count = rows if e == 0 else edge
-        source = src.at[:, pl.ds(rows - edge if e == 1 else 0, count), :]
+        source = src.at[pl.ds(plane, planes), pl.ds(rows - edge if e == 1 else 0, count), :]
         start = {0: edge, 1: 0, -1: edge + rows}[low_row]
-        target = dst.at[pl.ds(slot * lead, lead), pl.ds(start, count), :]
+        target = dst.at[pl.ds(slot * lead + plane, planes), pl.ds(start, count), :]
         k = (d + reach) * 3 + e + 1
         return pltpu.make_async_remote_copy(
             src_ref=source, dst_ref=target, send_sem=send.at[k], recv_sem=recv.at[slot * 3 + 1 - low_row],
             device_id=(gx + d, gy + e), device_id_type=MESH,
         )
 
-    def window(reach):
+    def window(low, high):
         for e in (0, 1, -1):
-            for d in sorted(range(-reach, reach + 1), key=abs):
-                if (d, e) != (0, 0):
+            for d in sorted(range(-high, high + 1), key=abs):
+                if (d, e) != (0, 0) and abs(d) >= low:
                     there = (gx + d >= 0) & (gx + d < ngx) & (gy + e >= 0) & (gy + e < ngy)
                     yield d, e, there
 
-    def window_send(src, dst, send, recv, reach, edge):
-        for d, e, there in window(reach):
+    def window_send(refs, low, high, half=None):
+        reach = refs[4]
+        for d, e, there in window(low, high):
             @pl.when(there)
             def _():
-                window_copy(src, dst, send, recv, reach, edge, d, e, reach - d, e).start()
-
-    def window_wait(src, dst, send, recv, reach, edge):
-        for d, e, there in window(reach):
+                window_copy(*refs, half, d, e, reach - d, e, d).start()
+
+    def window_wait(refs, low, high, half=None):
+        reach = refs[4]
+        for d, e, there in window(low, high):
             @pl.when(there)
             def _():
-                window_copy(src, dst, send, recv, reach, edge, d, e, reach + d, -e).wait_recv()
-
-    def window_done(src, dst, send, recv, reach, edge):
-        for d, e, there in window(reach):
+                window_copy(*refs, half, d, e, reach + d, -e, -d).wait_recv()
+
+    def window_done(refs, low, high, half=None):
+        reach = refs[4]
+        for d, e, there in window(low, high):
             @pl.when(there)
             def _():
-                window_copy(src, dst, send, recv, reach, edge, d, e, reach - d, e).wait_send()
+                window_copy(*refs, half, d, e, reach - d, e, d).wait_send()
 
     def gather_send(src, dst, k):
         def body(t, carry):
@@ -172,11 +179,12 @@
         )
 
     phase_window = (p_pack, wp, sp, rp, REACH, EDGE_PHASE)
-    fine_window = (f_ref, w0, s0, r0, 1, EDGE)
+    near_window = (f_ref, w0, s0, r0, 1, EDGE)
+    far_window = (f_ref, w0, sf, rf, 1, EDGE)
     coarse_window = (g1_pack, w1, s1, r1, REACH, EDGE)
-    window_send(*phase_window)
-    window_send(*fine_window)
-    gather_send(p_pack, gp, 0)
+    window_send(phase_window, 0, 1)
+    window_send(near_window, 0, 1, 0)
+    window_send(phase_window, 2, REACH)
 
     wp[REACH, pl.ds(EDGE_PHASE, by), :] = p_pack[0]
     gp[me] = p_pack[0]
@@ -243,49 +251,62 @@
         zh = harmonic(b, jnp.where(lane >= nz - step, 0.0, roll(b, -step, 1)))
         return yl, yh, zl, zh
 
-    window_wait(*phase_window)
-    for t in range(2 * REACH + 1):
+    def phase_block(t):
         packed = wp[t].astype(jnp.float32)[EDGE_PHASE - EDGE : EDGE_PHASE + by + EDGE]
         b1[2 * t] = even_part(packed, 1)
         b1[2 * t + 1] = odd_part(packed, 1)
 
-    level0 = level_refs[0]
+    window_wait(phase_window, 0, 1)
+    for t in range(REACH - 1, REACH + 2):
+        phase_block(t)
+
+    level0 = list(level_refs[0])
+    level0[2] = w0
     (va, vb, f0, inv0, c0, fx0) = level0[:6]
     rows0 = ly + 2 * EDGE
     blocks = 3 * lx // 2
     first_block = 2 * REACH - lx // 2
-    before = None
-    beta0 = []
-    for j in range(-1, blocks + 1):
-        stretch(b1[first_block + j], (j + 1) % slots)
-        b = temp[(j + 1) % slots, pl.ds(EDGE, rows0), :]
-        if before is not None:
-            fx0[2 * j] = harmonic(before, b)
-        if 0 <= j < blocks:
-            fx0[2 * j + 1] = b
-            beta0.append(b)
-        before = b
-    for j in range(blocks):
+    planes0 = 3 * lx
+    near0, near1 = lx - 2, 2 * lx + 2
+
+    def fine_beta(j):
+        slot = (j + 1) % slots
+        stretch(b1[first_block + j], slot)
+        return temp[slot, pl.ds(EDGE, rows0), :]
+
+    def fine_faces(j):
         lows = cell_faces(beta0[j], 1)
         for i in (2 * j, 2 * j + 1):
             put_faces(level0, i, beta0[j] > 0.0, lows, 1, None)
 
-    window_wait(*fine_window)
-    level0 = list(level0)
-    level0[2] = w0
-    planes0 = 3 * lx
-    for i in range(planes0):
+    beta0 = [fine_beta(j) for j in range(blocks)]
+    for j in range(blocks):
+        if j > 0:
+            fx0[2 * j] = harmonic(beta0[j - 1], beta0[j])
+        fx0[2 * j + 1] = beta0[j]
+    for j in range(near0 // 2, near1 // 2):
+        fine_faces(j)
+
+    window_wait(near_window, 0, 1, 0)
+    window_send(far_window, 1, 1, 1)
+    gather_send(p_pack, gp, 0)
+    for i in range(near0, near1):
         va[i + 1] = inv0[i] * w0[i]
-    sweep(level0, va, vb, 1, 1, planes0 - 1)
+    sweep(level0, va, vb, 1, near0 + 1, near1 - 1)
     rests = [rest_of(level0, vb, lx + i, 1)[EDGE : EDGE + ly] for i in range(lx)]
     coarse = [
         0.5 * pair_lanes(pair_rows(rests[2 * k] + rests[2 * k + 1], k % slots), 1) for k in range(lx // 2)
     ]
     packed = jnp.where(lane_bit(coarse[0], 1) == 0, coarse[0], coarse[1])
     g1_pack[0] = packed
-    window_send(*coarse_window)
+    window_send(coarse_window, 0, 1)
+    window_send(coarse_window, 2, REACH)
     w1[REACH, pl.ds(EDGE, by), :] = packed
 
+    window_wait(phase_window, 2, REACH)
+    for t in range(2 * REACH + 1):
+        if abs(t - REACH) > 1:
+            phase_block(t)
     level1 = level_refs[1]
     (ua, ub, f1, inv1, c1, fx1) = level1[:6]
     planes1 = 2 * (2 * REACH + 1)
@@ -369,20 +390,43 @@
 
         each(nx, finish)
 
-    window_wait(*coarse_window)
-    for t in range(2 * REACH + 1):
+    def coarse_block(t):
         f1[2 * t] = even_part(w1[t], 1)
         f1[2 * t + 1] = odd_part(w1[t], 1)
-    for i in range(planes1):
-        ua[i + 1] = inv1[i] * f1[i]
-    sweep(level1, ua, ub, 2, 1, planes1 - 1)
-    rests = [rest_of(level1, ub, 2 * REACH + i, 2)[EDGE : EDGE + by] for i in range(2)]
+        for i in (2 * t, 2 * t + 1):
+            ua[i + 1] = inv1[i] * f1[i]
+
+    own1 = 2 * REACH
+    window_wait(coarse_window, 0, 1)
+    for t in range(REACH - 1, REACH + 2):
+        coarse_block(t)
+    sweep(level1, ua, ub, 2, own1 - 1, own1 + 3)
+    rests = [rest_of(level1, ub, own1 + i, 2)[EDGE : EDGE + by] for i in range(2)]
     coarse = 0.5 * pair_lanes(pair_rows(rests[0] + rests[1], 0), 2)
     half = cy // 2
     packed = jnp.where(lane_bit(coarse[:half], 1) == 0, coarse[:half], coarse[half:])
     g2_pack[0] = packed
     gather_send(g2_pack, g2, 1)
     g2[me] = packed
+
+    window_wait(coarse_window, 2, REACH)
+    for t in range(2 * REACH + 1):
+        if abs(t - REACH) > 1:
+            coarse_block(t)
+    sweep(level1, ua, ub, 2, 1, own1 - 1)
+    sweep(level1, ua, ub, 2, own1 + 3, planes1 - 1)
+
+    fx0[0] = harmonic(fine_beta(-1), beta0[0])
+    fx0[planes0] = harmonic(beta0[blocks - 1], fine_beta(blocks))
+    window_wait(far_window, 1, 1, 1)
+    for j in range(blocks):
+        if not near0 <= 2 * j < near1:
+            fine_faces(j)
+            for i in (2 * j, 2 * j + 1):
+                va[i + 1] = inv0[i] * w0[i]
+    sweep(level0, va, vb, 1, 1, near0 + 1)
+    sweep(level0, va, vb, 1, near1 - 1, planes0 - 1)
+
     gather_all(g2, 1).wait_recv()
 
     f2 = level2[2]
@@ -479,9 +523,10 @@
         scaled_ref[i] = product[own]
         rest_ref[i] = w0[lx + i, pl.ds(EDGE, ly), :] - product[own] + near[own]
 
-    window_done(*phase_window)
-    window_done(*fine_window)
-    window_done(*coarse_window)
+    window_done(phase_window, 0, REACH)
+    window_done(near_window, 0, 1, 0)
+    window_done(far_window, 1, 1, 1)
+    window_done(coarse_window, 0, REACH)
     gather_all(gp, 0).wait_send()
     gather_all(g2, 1).wait_send()
 
@@ -522,7 +567,7 @@
         scratch += level_scratch(2 * blocks, by + 2 * EDGE)
         for l in range(2, LEVELS + 1):
             scratch += level_scratch(counts[l][0], max(counts[l][1], EDGE))
-        scratch += [pltpu.SemaphoreType.DMA((9,))] * 2
+        scratch += [pltpu.SemaphoreType.DMA((9,))] * 4
         scratch += [pltpu.SemaphoreType.DMA((3 * blocks,))] * 4
         scratch += [pltpu.SemaphoreType.DMA((2,))] * 2
         return pl.pallas_call(

time: 37.5 us -> 40.8 us (1.088)
  Pallas kernels: 34.4 us -> 37.7 us
    pallas_call x1, Pallas kernels: 34.4 us -> 37.7 us  [on_device(): pl.pallas_call(functools.partial(kernel, ngx, ngy, counts), out_shape=[ja...]
where the time goes in v2:
time: 40.8 us; the launch traced here: 40.6 us
  Pallas kernels  37.7 us (92%)
  local copies, waits for them, and re-layouts  2.26 us (6%)
  between operations  0.65 us (2%)
    pallas_call x1, Pallas kernels, on_device(): pl.pallas_call(functools.partial(kernel, ngx, ngy, counts), out_shape=[ja...  37.7 us
    unnamed x4, local copies, waits for them, and re-layouts  2.26 us

profile of v2, /device:TPU:0, one launch (start us, length us, event | category | flops | bytes accessed | tf_op | source)
XLA Modules:
  0.0 40.6 jit_solution(9874227425006600626)
XLA Ops:
  0.6 37.7 %shard_map.41 = (f32[4,64,128]{2,1,0:T(8,128)}, f32[4,64,128]{2,1,0:T(8,128)}) custom-call(f32[4,64,128]{2,1,0:T(8,128)} %f_ref.1, s32[4,64,128]{2,1,0:T(8,128)} %phase_ref.1), custom_call_target="tpu_custom_call" | custom-call | tf_op jit(solution)/shard_map/pallas_call | solution.py:573
  38.3 0.0 copy-start
  38.3 1.6 %copy.6 = f32[4,64,128]{2,1,0:T(8,128)} copy(f32[4,64,128]{2,1,0:T(8,128)} %get-tuple-element.4) | data formatting | bytes 262144
  39.9 0.0 copy-done
  39.9 0.7 %copy.7 = f32[4,64,128]{2,1,0:T(8,128)} copy(f32[4,64,128]{2,1,0:T(8,128)S(1)} %copy-done) | data formatting | bytes 262144
Async XLA Ops:
  38.3 1.6 %copy-start = (f32[4,64,128]{2,1,0:T(8,128)S(1)}, f32[4,64,128]{2,1,0:T(8,128)}, u32[]{:S(2)}) copy-start(f32[4,64,128]{2,1,0:T(8,128)} %get-tuple-element.5) | copy-start | bytes 393220
